TPU v7x, 512 devices: a whole 4x8x8 slice. The times are simulated.
512 devices in a mesh: gx: 16 (over x_lo, z), gy: 32 (over x_hi, y, core).
Axes of the slice: x: 4 (x_hi: 2, x_lo: 2; x = x_hi * 2 + x_lo), y: 8, z: 8, core: 2. Of those that a mesh axis runs over, the one named last changes fastest.
Arguments:
- state: float32 [8, 2, 64, 16256], P(None, None, 'gx', 'gy'), may hold values from -1 to 5, as said below
- shear_offset: int32 [1], replicated, may hold values from 0 to 16255
- remap_shift: int32 [64], P('gx'), may hold values from 0 to 16255
- frac_index: int32 [64], P('gx'), may hold values from 0 to 15
Outputs:
- new_state: float32 [8, 2, 64, 16256], P(None, None, 'gx', 'gy')
Inputs may be any that keep to these rules, and one draw needn't show every extreme that they name: `state`: field 0 lies in 0.5 to 2, fields 1 to 3 and 5 to 7 within 1 in magnitude, field 4 in 1 to 5.
All inputs are finite; a program needn't handle non-finite values.
Results may differ from a plain program's by a relative error of at most 0.00002.
Values sent between devices are 32-bit elements; how exact they have to be, the bound alone decides.
A program may use at most 64 MiB of HBM per device.

v0:
```python
import jax
import jax.numpy as jnp
from jax import lax
from jax.sharding import PartitionSpec as P

FRAC = 16


ADIABATIC = 5.0 / 3.0
ROTATION = 1.0
SHEAR_RATE = 1.5
MAX_SPEED = 5.0
TIME_STEP = 0.05


def with_halo(array, sides, width):
    for axis, dim in sides:
        peers, length = (lax.axis_size(axis), array.shape[dim])
        up = [(i, (i + 1) % peers) for i in range(peers)]
        down = [(j, i) for i, j in up]
        last = lax.slice_in_dim(array, length - width, length, axis=dim)
        leading = lax.slice_in_dim(array, 0, width, axis=dim)
        before = lax.ppermute(last, axis, up)
        after = lax.ppermute(leading, axis, down)
        array = jnp.concatenate([before, array, after], axis=dim)
    return array


def shifted_2(block, axis, distance):
    devices = range(lax.axis_size(axis))
    route = [((i - distance) % len(devices), i) for i in devices]
    return lax.ppermute(block, axis, route)


def next_cell(value, grid_axis):
    return jnp.roll(value, -1, grid_axis)


def prev_cell(value, grid_axis):
    return jnp.roll(value, 1, grid_axis)


def tendency(state):
    density, mom_x, mom_y, mom_z, energy, face_x, face_y, face_z = state
    cen_x = 0.5 * (face_x + next_cell(face_x, 1))
    cen_y = 0.5 * (face_y + next_cell(face_y, 2))
    cen_z = 0.5 * (face_z + next_cell(face_z, 0))
    vel_x = mom_x / density
    vel_y = mom_y / density
    vel_z = mom_z / density
    magnetic = 0.5 * (cen_x * cen_x + cen_y * cen_y + cen_z * cen_z)
    pressure = (ADIABATIC - 1.0) * (
        energy - 0.5 * (mom_x * vel_x + mom_y * vel_y + mom_z * vel_z) - magnetic
    ) + magnetic
    vel_dot = vel_x * cen_x + vel_y * cen_y + vel_z * cen_z
    conserved = (density, mom_x, mom_y, mom_z, energy)
    momenta = (mom_x, mom_y, mom_z)
    centred = (cen_x, cen_y, cen_z)
    velocity = (vel_x, vel_y, vel_z)
    change = [jnp.zeros_like(density) for member in range(5)]
    for normal, grid_axis in ((0, 1), (1, 2), (2, 0)):
        normal_speed = velocity[normal]
        across = centred[normal]
        fluxes = [momenta[normal]]
        for second in range(3):
            flux_term = momenta[second] * normal_speed - across * centred[second]
            if second == normal:
                flux_term = flux_term + pressure
            fluxes.append(flux_term)
        fluxes.append((energy + pressure) * normal_speed - across * vel_dot)
        for member in range(5):
            upwind = 0.5 * (
                prev_cell(fluxes[member], grid_axis) + fluxes[member]
            ) - 0.5 * MAX_SPEED * (conserved[member] - prev_cell(conserved[member], grid_axis))
            change[member] = change[member] - (next_cell(upwind, grid_axis) - upwind)
    change[1] = change[1] + 2.0 * ROTATION * mom_y
    change[2] = change[2] - (2.0 - SHEAR_RATE) * ROTATION * mom_x
    change[4] = change[4] + SHEAR_RATE * ROTATION * (mom_x * vel_y - cen_x * cen_y)
    elec_x = -(vel_y * cen_z - vel_z * cen_y)
    elec_y = -(vel_z * cen_x - vel_x * cen_z)
    elec_z = -(vel_x * cen_y - vel_y * cen_x)
    edge_x = 0.25 * (
        elec_x + prev_cell(elec_x, 2) + prev_cell(elec_x, 0) + prev_cell(prev_cell(elec_x, 2), 0)
    )
    edge_y = 0.25 * (
        elec_y + prev_cell(elec_y, 1) + prev_cell(elec_y, 0) + prev_cell(prev_cell(elec_y, 1), 0)
    )
    edge_z = 0.25 * (
        elec_z + prev_cell(elec_z, 1) + prev_cell(elec_z, 2) + prev_cell(prev_cell(elec_z, 1), 2)
    )
    delta_x = -(next_cell(edge_z, 2) - edge_z - (next_cell(edge_y, 0) - edge_y))
    delta_y = -(next_cell(edge_x, 0) - edge_x - (next_cell(edge_z, 1) - edge_z))
    delta_z = -(next_cell(edge_y, 1) - edge_y - (next_cell(edge_x, 2) - edge_x))
    return jnp.stack(change + [delta_x, delta_y, delta_z])


def fill_ghosts(state, width, offset):
    padded = with_halo(state, (("gx", 2),), width)
    left_strip = padded[:, :, :width, :]
    right_strip = padded[:, :, -width:, :]
    cells = state.shape[3]
    devices = lax.axis_size("gy")
    total = cells * devices
    amounts = (offset, (total - offset) % total)
    hop_counts = [amount // cells for amount in amounts]
    remainders = [amount % cells for amount in amounts]
    moved = (left_strip, right_strip)
    for bit_pos in range(devices.bit_length() - 1):
        shifted = shifted_2((moved[0], moved[1]), "gy", 1 << bit_pos)
        moved = tuple(
            (
                jnp.where(
                    hop_counts[member] // (1 << bit_pos) % 2 == 1, shifted[member], moved[member]
                )
                for member in range(2)
            )
        )
    earlier = shifted_2((moved[0], moved[1]), "gy", 1)
    windows = []
    for member in range(2):
        joined = jnp.concatenate([earlier[member], moved[member]], axis=3)
        windows.append(lax.dynamic_slice_in_dim(joined, cells - remainders[member], cells, axis=3))
    place = lax.axis_index("gx")
    new_left = jnp.where(place == 0, windows[0], left_strip)
    new_right = jnp.where(place == lax.axis_size("gx") - 1, windows[1], right_strip)
    radial = jnp.concatenate([new_left, padded[:, :, width:-width, :], new_right], axis=2)
    return with_halo(radial, (("gy", 3),), width)


def shards(state, shear_offset, remap_shift, frac_index):
    offset = shear_offset[0]
    first = state + TIME_STEP * tendency(fill_ghosts(state, 2, offset))[:, :, 2:-2, 2:-2]
    advanced = 0.5 * (
        state + (first + TIME_STEP * tendency(fill_ghosts(first, 2, offset))[:, :, 2:-2, 2:-2])
    )
    fraction = (frac_index.astype(jnp.float32) + 0.5) / FRAC
    cells = advanced.shape[3]
    hop_counts = remap_shift // cells
    remainders = remap_shift % cells
    moved = advanced
    for bit_pos in range(lax.axis_size("gy").bit_length() - 1):
        shifted = shifted_2(moved, "gy", 1 << bit_pos)
        chosen = (hop_counts // (1 << bit_pos) % 2 == 1)[:, None]
        moved = jnp.where(chosen, shifted, moved)
    earlier = shifted_2(moved, "gy", 1)
    joined = jnp.concatenate([earlier, moved], axis=3)
    outputs = []
    for row_pos in range(joined.shape[2]):
        start = cells - 1 - remainders[row_pos]
        window = lax.dynamic_slice_in_dim(joined[:, :, row_pos, :], start, cells + 1, axis=2)
        weight = fraction[row_pos]
        outputs.append((1.0 - weight) * window[:, :, 1:] + weight * window[:, :, :-1])
    return jnp.stack(outputs, axis=2)


def solution(mesh):
    placed = (P(None, None, "gx", "gy"), P(), P("gx"), P("gx"))
    return jax.shard_map(
        shards, mesh=mesh, in_specs=placed, out_specs=P(None, None, "gx", "gy"), check_vma=False
    )
```

profile of v0, /device:TPU:57, one launch (start us, length us, event | category | flops | bytes accessed | tf_op | source)
XLA Modules:
  0.0 256.4 jit_solution(10137278645853941790)
XLA Ops:
  0.0 1.0 fusion.335
  1.0 11.6 %collective-permute-start.7 = (f32[8,2,2,508]{3,2,1,0:T(2,128)S(1)}, f32[8,2,2,508]{3,2,1,0:T(2,128)S(1)}, u32[]{:S(2)}, u32[]{:S(2)}) collective-permute-start(f32[8,2,2,508]{3,2,1,0:T(2,128)S(1)} %get-tuple-element.186), channel_id=1, source_target_pairs={{32,0},{64,32},{96,64},{128,96},{160,128},{192,160},{224,192},{256... | collective-permute-start | bytes 195080 | tf_op jit(solution)/shard_map/ppermute | solution.py:24
  12.6 1.9 collective-permute-start
  14.6 4.4 %collective-permute-start.8 = (f32[8,2,2,508]{3,2,1,0:T(2,128)S(1)}, f32[8,2,2,508]{3,2,1,0:T(2,128)S(1)}, u32[]{:S(2)}, u32[]{:S(2)}) collective-permute-start(f32[8,2,2,508]{3,2,1,0:T(2,128)S(1)} %collective-permute-done.7), channel_id=1, source_target_pairs={{31,0},{0,1},{1,2},{2,3},{3,4},{4,5},{5,6},{6,7},{7,8},{8,9},{9,10... | collective-permute-start | bytes 195080 | tf_op jit(solution)/shard_map/ppermute | solution.py:32
  20.0 5.3 %collective-permute-start.1 = (f32[8,2,2,508]{3,2,1,0:T(2,128)S(1)}, f32[8,2,2,508]{3,2,1,0:T(2,128)S(1)}, u32[]{:S(2)}, u32[]{:S(2)}) collective-permute-start(f32[8,2,2,508]{3,2,1,0:T(2,128)S(1)} %collective-permute-done), channel_id=1, source_target_pairs={{31,0},{0,1},{1,2},{2,3},{3,4},{4,5},{5,6},{6,7},{7,8},{8,9},{9,10... | collective-permute-start | bytes 195080 | tf_op jit(solution)/shard_map/ppermute | solution.py:32
  25.4 3.2 %collective-permute-start.9 = (f32[8,2,2,508]{3,2,1,0:T(2,128)S(1)}, f32[8,2,2,508]{3,2,1,0:T(2,128)S(1)}, u32[]{:S(2)}, u32[]{:S(2)}) collective-permute-start(f32[8,2,2,508]{3,2,1,0:T(2,128)S(1)} %broadcast_select_fusion.6), channel_id=1, source_target_pairs={{30,0},{31,1},{0,2},{1,3},{2,4},{3,5},{4,6},{5,7},{6,8},{7,9},{8,1... | collective-permute-start | bytes 195080 | tf_op jit(solution)/shard_map/ppermute | solution.py:32
  28.6 3.2 %collective-permute-start.2 = (f32[8,2,2,508]{3,2,1,0:T(2,128)S(1)}, f32[8,2,2,508]{3,2,1,0:T(2,128)S(1)}, u32[]{:S(2)}, u32[]{:S(2)}) collective-permute-start(f32[8,2,2,508]{3,2,1,0:T(2,128)S(1)} %broadcast_select_fusion.16), channel_id=1, source_target_pairs={{30,0},{31,1},{0,2},{1,3},{2,4},{3,5},{4,6},{5,7},{6,8},{7,9},{8,1... | collective-permute-start | bytes 195080 | tf_op jit(solution)/shard_map/ppermute | solution.py:32
  31.9 5.4 %collective-permute-start.10 = (f32[8,2,2,508]{3,2,1,0:T(2,128)S(1)}, f32[8,2,2,508]{3,2,1,0:T(2,128)S(1)}, u32[]{:S(2)}, u32[]{:S(2)}) collective-permute-start(f32[8,2,2,508]{3,2,1,0:T(2,128)S(1)} %broadcast_select_fusion.8), channel_id=1, source_target_pairs={{28,0},{29,1},{30,2},{31,3},{0,4},{1,5},{2,6},{3,7},{4,8},{5,9},{6... | collective-permute-start | bytes 195080 | tf_op jit(solution)/shard_map/ppermute | solution.py:32
  37.4 2.7 %collective-permute-start.3 = (f32[8,2,2,508]{3,2,1,0:T(2,128)S(1)}, f32[8,2,2,508]{3,2,1,0:T(2,128)S(1)}, u32[]{:S(2)}, u32[]{:S(2)}) collective-permute-start(f32[8,2,2,508]{3,2,1,0:T(2,128)S(1)} %broadcast_select_fusion.18), channel_id=1, source_target_pairs={{28,0},{29,1},{30,2},{31,3},{0,4},{1,5},{2,6},{3,7},{4,8},{5,9},{6... | collective-permute-start | bytes 195080 | tf_op jit(solution)/shard_map/ppermute | solution.py:32
  40.2 3.6 %collective-permute-start.11 = (f32[8,2,2,508]{3,2,1,0:T(2,128)S(1)}, f32[8,2,2,508]{3,2,1,0:T(2,128)S(1)}, u32[]{:S(2)}, u32[]{:S(2)}) collective-permute-start(f32[8,2,2,508]{3,2,1,0:T(2,128)S(1)} %broadcast_select_fusion.10), channel_id=1, source_target_pairs={{24,0},{25,1},{26,2},{27,3},{28,4},{29,5},{30,6},{31,7},{0,8},{1,9... | collective-permute-start | bytes 195080 | tf_op jit(solution)/shard_map/ppermute | solution.py:32
  43.8 0.4 collective-permute-done.3
  44.3 5.4 %collective-permute-start.4 = (f32[8,2,2,508]{3,2,1,0:T(2,128)S(1)}, f32[8,2,2,508]{3,2,1,0:T(2,128)S(1)}, u32[]{:S(2)}, u32[]{:S(2)}) collective-permute-start(f32[8,2,2,508]{3,2,1,0:T(2,128)S(1)} %broadcast_select_fusion.20), channel_id=1, source_target_pairs={{24,0},{25,1},{26,2},{27,3},{28,4},{29,5},{30,6},{31,7},{0,8},{1,9... | collective-permute-start | bytes 195080 | tf_op jit(solution)/shard_map/ppermute | solution.py:32
  49.8 4.4 %collective-permute-start.12 = (f32[8,2,2,508]{3,2,1,0:T(2,128)S(1)}, f32[8,2,2,508]{3,2,1,0:T(2,128)S(1)}, u32[]{:S(2)}, u32[]{:S(2)}) collective-permute-start(f32[8,2,2,508]{3,2,1,0:T(2,128)S(1)} %broadcast_select_fusion.12), channel_id=1, source_target_pairs={{16,0},{17,1},{18,2},{19,3},{20,4},{21,5},{22,6},{23,7},{24,8},{25... | collective-permute-start | bytes 195080 | tf_op jit(solution)/shard_map/ppermute | solution.py:32
  54.2 3.9 %collective-permute-start.5 = (f32[8,2,2,508]{3,2,1,0:T(2,128)S(1)}, f32[8,2,2,508]{3,2,1,0:T(2,128)S(1)}, u32[]{:S(2)}, u32[]{:S(2)}) collective-permute-start(f32[8,2,2,508]{3,2,1,0:T(2,128)S(1)} %broadcast_select_fusion.22), channel_id=1, source_target_pairs={{16,0},{17,1},{18,2},{19,3},{20,4},{21,5},{22,6},{23,7},{24,8},{25... | collective-permute-start | bytes 195080 | tf_op jit(solution)/shard_map/ppermute | solution.py:32
  58.1 12.9 %collective-permute-start.13 = (f32[8,2,2,508]{3,2,1,0:T(2,128)S(1)}, f32[8,2,2,508]{3,2,1,0:T(2,128)S(1)}, u32[]{:S(2)}, u32[]{:S(2)}) collective-permute-start(f32[8,2,2,508]{3,2,1,0:T(2,128)S(1)} %broadcast_select_fusion.14), channel_id=1, source_target_pairs={{31,0},{0,1},{1,2},{2,3},{3,4},{4,5},{5,6},{6,7},{7,8},{8,9},{9,10... | collective-permute-start | bytes 195080 | tf_op jit(solution)/shard_map/ppermute | solution.py:32
  71.1 4.3 %collective-permute-start.6 = (f32[8,2,2,508]{3,2,1,0:T(2,128)S(1)}, f32[8,2,2,508]{3,2,1,0:T(2,128)S(1)}, u32[]{:S(2)}, u32[]{:S(2)}) collective-permute-start(f32[8,2,2,508]{3,2,1,0:T(2,128)S(1)} %broadcast_select_fusion.24), channel_id=1, source_target_pairs={{31,0},{0,1},{1,2},{2,3},{3,4},{4,5},{5,6},{6,7},{7,8},{8,9},{9,10... | collective-permute-start | bytes 195080 | tf_op jit(solution)/shard_map/ppermute | solution.py:32
  75.4 0.2 fusion.9
  75.7 1.1 collective-permute-done.6
  77.1 1.9 collective-permute-start.15
  79.0 7.9 %collective-permute-start.14 = (f32[8,2,8,2]{3,2,1,0:T(8,128)S(1)}, f32[8,2,8,2]{3,2,1,0:T(8,128)S(1)}, u32[]{:S(2)}, u32[]{:S(2)}) collective-permute-start(f32[8,2,8,2]{3,2,1,0:T(8,128)S(1)} %get-tuple-element.173), channel_id=1, source_target_pairs={{0,1},{1,2},{2,3},{3,4},{4,5},{5,6},{6,7},{7,8},{8,9},{9,10},{10,1... | collective-permute-start | bytes 3080 | tf_op jit(solution)/shard_map/ppermute | solution.py:23
  86.9 1.3 collective-permute-done.14
  88.2 0.3 pad_maximum_fusion
  92.7 3.5 %collective-permute-start.23 = (f32[8,2,2,508]{3,2,1,0:T(2,128)S(1)}, f32[8,2,2,508]{3,2,1,0:T(2,128)S(1)}, u32[]{:S(2)}, u32[]{:S(2)}) collective-permute-start(f32[8,2,2,508]{3,2,1,0:T(2,128)S(1)} %get-tuple-element.184), channel_id=1, source_target_pairs={{32,0},{64,32},{96,64},{128,96},{160,128},{192,160},{224,192},{256... | collective-permute-start | bytes 195080 | tf_op jit(solution)/shard_map/ppermute | solution.py:24
  96.2 1.9 collective-permute-start.16
  98.1 8.8 %collective-permute-start.24 = (f32[8,2,2,508]{3,2,1,0:T(2,128)S(1)}, f32[8,2,2,508]{3,2,1,0:T(2,128)S(1)}, u32[]{:S(2)}, u32[]{:S(2)}) collective-permute-start(f32[8,2,2,508]{3,2,1,0:T(2,128)S(1)} %collective-permute-done.23), channel_id=1, source_target_pairs={{31,0},{0,1},{1,2},{2,3},{3,4},{4,5},{5,6},{6,7},{7,8},{8,9},{9,10... | collective-permute-start | bytes 195080 | tf_op jit(solution)/shard_map/ppermute | solution.py:32
  106.9 6.3 %collective-permute-start.17 = (f32[8,2,2,508]{3,2,1,0:T(2,128)S(1)}, f32[8,2,2,508]{3,2,1,0:T(2,128)S(1)}, u32[]{:S(2)}, u32[]{:S(2)}) collective-permute-start(f32[8,2,2,508]{3,2,1,0:T(2,128)S(1)} %collective-permute-done.16), channel_id=1, source_target_pairs={{31,0},{0,1},{1,2},{2,3},{3,4},{4,5},{5,6},{6,7},{7,8},{8,9},{9,10... | collective-permute-start | bytes 195080 | tf_op jit(solution)/shard_map/ppermute | solution.py:32
  113.3 1.9 collective-permute-start.25
  115.2 1.9 collective-permute-start.18
  117.2 1.1 collective-permute-done.25
  118.3 1.9 collective-permute-start.26
  120.3 1.9 collective-permute-start.19
  122.2 2.7 %collective-permute-done.26 = f32[8,2,2,508]{3,2,1,0:T(2,128)S(1)} collective-permute-done((f32[8,2,2,508]{3,2,1,0:T(2,128)S(1)}, f32[8,2,2,508]{3,2,1,0:T(2,128)S(1)}, u32[]{:S(2)}, u32[]{:S(2)}) %collective-permute-start.26) | collective-permute-done | bytes 65056 | tf_op jit(solution)/shard_map/ppermute | solution.py:32
  125.0 5.8 %collective-permute-start.27 = (f32[8,2,2,508]{3,2,1,0:T(2,128)S(1)}, f32[8,2,2,508]{3,2,1,0:T(2,128)S(1)}, u32[]{:S(2)}, u32[]{:S(2)}) collective-permute-start(f32[8,2,2,508]{3,2,1,0:T(2,128)S(1)} %broadcast_select_fusion.9), channel_id=1, source_target_pairs={{24,0},{25,1},{26,2},{27,3},{28,4},{29,5},{30,6},{31,7},{0,8},{1,9... | collective-permute-start | bytes 195080 | tf_op jit(solution)/shard_map/ppermute | solution.py:32
  130.8 4.4 %collective-permute-start.20 = (f32[8,2,2,508]{3,2,1,0:T(2,128)S(1)}, f32[8,2,2,508]{3,2,1,0:T(2,128)S(1)}, u32[]{:S(2)}, u32[]{:S(2)}) collective-permute-start(f32[8,2,2,508]{3,2,1,0:T(2,128)S(1)} %broadcast_select_fusion.19), channel_id=1, source_target_pairs={{24,0},{25,1},{26,2},{27,3},{28,4},{29,5},{30,6},{31,7},{0,8},{1,9... | collective-permute-start | bytes 195080 | tf_op jit(solution)/shard_map/ppermute | solution.py:32
  135.3 3.6 %collective-permute-start.28 = (f32[8,2,2,508]{3,2,1,0:T(2,128)S(1)}, f32[8,2,2,508]{3,2,1,0:T(2,128)S(1)}, u32[]{:S(2)}, u32[]{:S(2)}) collective-permute-start(f32[8,2,2,508]{3,2,1,0:T(2,128)S(1)} %broadcast_select_fusion.11), channel_id=1, source_target_pairs={{16,0},{17,1},{18,2},{19,3},{20,4},{21,5},{22,6},{23,7},{24,8},{25... | collective-permute-start | bytes 195080 | tf_op jit(solution)/shard_map/ppermute | solution.py:32
  138.9 1.4 collective-permute-done.20
  140.3 3.1 %collective-permute-start.21 = (f32[8,2,2,508]{3,2,1,0:T(2,128)S(1)}, f32[8,2,2,508]{3,2,1,0:T(2,128)S(1)}, u32[]{:S(2)}, u32[]{:S(2)}) collective-permute-start(f32[8,2,2,508]{3,2,1,0:T(2,128)S(1)} %broadcast_select_fusion.21), channel_id=1, source_target_pairs={{16,0},{17,1},{18,2},{19,3},{20,4},{21,5},{22,6},{23,7},{24,8},{25... | collective-permute-start | bytes 195080 | tf_op jit(solution)/shard_map/ppermute | solution.py:32
  143.5 15.5 %collective-permute-start.29 = (f32[8,2,2,508]{3,2,1,0:T(2,128)S(1)}, f32[8,2,2,508]{3,2,1,0:T(2,128)S(1)}, u32[]{:S(2)}, u32[]{:S(2)}) collective-permute-start(f32[8,2,2,508]{3,2,1,0:T(2,128)S(1)} %broadcast_select_fusion.13), channel_id=1, source_target_pairs={{31,0},{0,1},{1,2},{2,3},{3,4},{4,5},{5,6},{6,7},{7,8},{8,9},{9,10... | collective-permute-start | bytes 195080 | tf_op jit(solution)/shard_map/ppermute | solution.py:32
  159.0 4.2 %collective-permute-start.22 = (f32[8,2,2,508]{3,2,1,0:T(2,128)S(1)}, f32[8,2,2,508]{3,2,1,0:T(2,128)S(1)}, u32[]{:S(2)}, u32[]{:S(2)}) collective-permute-start(f32[8,2,2,508]{3,2,1,0:T(2,128)S(1)} %broadcast_select_fusion.23), channel_id=1, source_target_pairs={{31,0},{0,1},{1,2},{2,3},{3,4},{4,5},{5,6},{6,7},{7,8},{8,9},{9,10... | collective-permute-start | bytes 195080 | tf_op jit(solution)/shard_map/ppermute | solution.py:32
  163.5 1.1 collective-permute-done.22
  164.9 1.9 collective-permute-start.31
  166.9 7.9 %collective-permute-start.30 = (f32[8,2,8,2]{3,2,1,0:T(8,128)S(1)}, f32[8,2,8,2]{3,2,1,0:T(8,128)S(1)}, u32[]{:S(2)}, u32[]{:S(2)}) collective-permute-start(f32[8,2,8,2]{3,2,1,0:T(8,128)S(1)} %get-tuple-element.131), channel_id=1, source_target_pairs={{0,1},{1,2},{2,3},{3,4},{4,5},{5,6},{6,7},{7,8},{8,9},{9,10},{10,1... | collective-permute-start | bytes 3080 | tf_op jit(solution)/shard_map/ppermute | solution.py:23
  174.8 1.3 collective-permute-done.30
  176.1 0.3 pad_maximum_fusion.1
  180.8 7.9 %collective-permute-start.32 = (f32[8,2,4,508]{3,2,1,0:T(4,128)S(1)}, f32[8,2,4,508]{3,2,1,0:T(4,128)S(1)}, u32[]{:S(2)}, u32[]{:S(2)}) collective-permute-start(f32[8,2,4,508]{3,2,1,0:T(4,128)S(1)} %fusion.2), channel_id=1, source_target_pairs={{31,0},{0,1},{1,2},{2,3},{3,4},{4,5},{5,6},{6,7},{7,8},{8,9},{9,10... | collective-permute-start | bytes 390152 | tf_op jit(solution)/shard_map/ppermute | solution.py:32
  188.7 1.9 collective-permute-done.32
  190.7 1.9 collective-permute-start.33
  192.6 3.8 %collective-permute-done.33 = f32[8,2,4,508]{3,2,1,0:T(4,128)S(1)} collective-permute-done((f32[8,2,4,508]{3,2,1,0:T(4,128)S(1)}, f32[8,2,4,508]{3,2,1,0:T(4,128)S(1)}, u32[]{:S(2)}, u32[]{:S(2)}) %collective-permute-start.33) | collective-permute-done | bytes 130080 | tf_op jit(solution)/shard_map/ppermute | solution.py:32
  196.5 1.9 collective-permute-start.34
  198.5 5.5 %collective-permute-done.34 = f32[8,2,4,508]{3,2,1,0:T(4,128)S(1)} collective-permute-done((f32[8,2,4,508]{3,2,1,0:T(4,128)S(1)}, f32[8,2,4,508]{3,2,1,0:T(4,128)S(1)}, u32[]{:S(2)}, u32[]{:S(2)}) %collective-permute-start.34) | collective-permute-done | bytes 130080 | tf_op jit(solution)/shard_map/ppermute | solution.py:32
  204.0 1.9 collective-permute-start.35
  206.0 7.7 %collective-permute-done.35 = f32[8,2,4,508]{3,2,1,0:T(4,128)S(1)} collective-permute-done((f32[8,2,4,508]{3,2,1,0:T(4,128)S(1)}, f32[8,2,4,508]{3,2,1,0:T(4,128)S(1)}, u32[]{:S(2)}, u32[]{:S(2)}) %collective-permute-start.35) | collective-permute-done | bytes 130080 | tf_op jit(solution)/shard_map/ppermute | solution.py:32
  213.8 3.3 %collective-permute-start.36 = (f32[8,2,4,508]{3,2,1,0:T(4,128)S(1)}, f32[8,2,4,508]{3,2,1,0:T(4,128)S(1)}, u32[]{:S(2)}, u32[]{:S(2)}) collective-permute-start(f32[8,2,4,508]{3,2,1,0:T(4,128)S(1)} %broadcast_select_fusion.3), channel_id=1, source_target_pairs={{16,0},{17,1},{18,2},{19,3},{20,4},{21,5},{22,6},{23,7},{24,8},{25... | collective-permute-start | bytes 390152 | tf_op jit(solution)/shard_map/ppermute | solution.py:32
  217.1 0.6 fusion.337
  217.7 3.3 %collective-permute-done.36 = f32[8,2,4,508]{3,2,1,0:T(4,128)S(1)} collective-permute-done((f32[8,2,4,508]{3,2,1,0:T(4,128)S(1)}, f32[8,2,4,508]{3,2,1,0:T(4,128)S(1)}, u32[]{:S(2)}, u32[]{:S(2)}) %collective-permute-start.36) | collective-permute-done | bytes 130080 | tf_op jit(solution)/shard_map/ppermute | solution.py:32
  221.1 22.5 %collective-permute-start.37 = (f32[8,2,4,508]{3,2,1,0:T(4,128)S(1)}, f32[8,2,4,508]{3,2,1,0:T(4,128)S(1)}, u32[]{:S(2)}, u32[]{:S(2)}) collective-permute-start(f32[8,2,4,508]{3,2,1,0:T(4,128)S(1)} %broadcast_select_fusion.4), channel_id=1, source_target_pairs={{31,0},{0,1},{1,2},{2,3},{3,4},{4,5},{5,6},{6,7},{7,8},{8,9},{9,10... | collective-permute-start | bytes 390152 | tf_op jit(solution)/shard_map/ppermute | solution.py:32
  243.6 0.7 fusion.336
  251.4 0.3 pad_slice_fusion.1
  251.7 0.2 fusion.12
  252.8 0.6 fusion.40
  253.4 0.7 fusion.42
  254.2 0.8 fusion.44
  254.9 0.7 fusion.46
  255.6 0.7 copy.179
  (299 shorter events, 10.6 us)
Async XLA Ops:
  1.0 13.5 %collective-permute-start.7 = (f32[8,2,2,508]{3,2,1,0:T(2,128)S(1)}, f32[8,2,2,508]{3,2,1,0:T(2,128)S(1)}, u32[]{:S(2)}, u32[]{:S(2)}) collective-permute-start(f32[8,2,2,508]{3,2,1,0:T(2,128)S(1)} %get-tuple-element.186), channel_id=1, source_target_pairs={{32,0},{64,32},{96,64},{128,96},{160,128},{192,160},{224,192},{256... | collective-permute-start | bytes 195080 | tf_op jit(solution)/shard_map/ppermute | solution.py:24
  12.6 7.4 %collective-permute-start = (f32[8,2,2,508]{3,2,1,0:T(2,128)S(1)}, f32[8,2,2,508]{3,2,1,0:T(2,128)S(1)}, u32[]{:S(2)}, u32[]{:S(2)}) collective-permute-start(f32[8,2,2,508]{3,2,1,0:T(2,128)S(1)} %get-tuple-element.185), channel_id=1, source_target_pairs={{0,32},{32,64},{64,96},{96,128},{128,160},{160,192},{192,224},{224... | collective-permute-start | bytes 195080 | tf_op jit(solution)/shard_map/ppermute | solution.py:23
  14.6 10.7 %collective-permute-start.8 = (f32[8,2,2,508]{3,2,1,0:T(2,128)S(1)}, f32[8,2,2,508]{3,2,1,0:T(2,128)S(1)}, u32[]{:S(2)}, u32[]{:S(2)}) collective-permute-start(f32[8,2,2,508]{3,2,1,0:T(2,128)S(1)} %collective-permute-done.7), channel_id=1, source_target_pairs={{31,0},{0,1},{1,2},{2,3},{3,4},{4,5},{5,6},{6,7},{7,8},{8,9},{9,10... | collective-permute-start | bytes 195080 | tf_op jit(solution)/shard_map/ppermute | solution.py:32
  20.0 8.6 %collective-permute-start.1 = (f32[8,2,2,508]{3,2,1,0:T(2,128)S(1)}, f32[8,2,2,508]{3,2,1,0:T(2,128)S(1)}, u32[]{:S(2)}, u32[]{:S(2)}) collective-permute-start(f32[8,2,2,508]{3,2,1,0:T(2,128)S(1)} %collective-permute-done), channel_id=1, source_target_pairs={{31,0},{0,1},{1,2},{2,3},{3,4},{4,5},{5,6},{6,7},{7,8},{8,9},{9,10... | collective-permute-start | bytes 195080 | tf_op jit(solution)/shard_map/ppermute | solution.py:32
  25.4 6.5 %collective-permute-start.9 = (f32[8,2,2,508]{3,2,1,0:T(2,128)S(1)}, f32[8,2,2,508]{3,2,1,0:T(2,128)S(1)}, u32[]{:S(2)}, u32[]{:S(2)}) collective-permute-start(f32[8,2,2,508]{3,2,1,0:T(2,128)S(1)} %broadcast_select_fusion.6), channel_id=1, source_target_pairs={{30,0},{31,1},{0,2},{1,3},{2,4},{3,5},{4,6},{5,7},{6,8},{7,9},{8,1... | collective-permute-start | bytes 195080 | tf_op jit(solution)/shard_map/ppermute | solution.py:32
  28.6 8.7 %collective-permute-start.2 = (f32[8,2,2,508]{3,2,1,0:T(2,128)S(1)}, f32[8,2,2,508]{3,2,1,0:T(2,128)S(1)}, u32[]{:S(2)}, u32[]{:S(2)}) collective-permute-start(f32[8,2,2,508]{3,2,1,0:T(2,128)S(1)} %broadcast_select_fusion.16), channel_id=1, source_target_pairs={{30,0},{31,1},{0,2},{1,3},{2,4},{3,5},{4,6},{5,7},{6,8},{7,9},{8,1... | collective-permute-start | bytes 195080 | tf_op jit(solution)/shard_map/ppermute | solution.py:32
  31.9 8.2 %collective-permute-start.10 = (f32[8,2,2,508]{3,2,1,0:T(2,128)S(1)}, f32[8,2,2,508]{3,2,1,0:T(2,128)S(1)}, u32[]{:S(2)}, u32[]{:S(2)}) collective-permute-start(f32[8,2,2,508]{3,2,1,0:T(2,128)S(1)} %broadcast_select_fusion.8), channel_id=1, source_target_pairs={{28,0},{29,1},{30,2},{31,3},{0,4},{1,5},{2,6},{3,7},{4,8},{5,9},{6... | collective-permute-start | bytes 195080 | tf_op jit(solution)/shard_map/ppermute | solution.py:32
  37.4 6.9 %collective-permute-start.3 = (f32[8,2,2,508]{3,2,1,0:T(2,128)S(1)}, f32[8,2,2,508]{3,2,1,0:T(2,128)S(1)}, u32[]{:S(2)}, u32[]{:S(2)}) collective-permute-start(f32[8,2,2,508]{3,2,1,0:T(2,128)S(1)} %broadcast_select_fusion.18), channel_id=1, source_target_pairs={{28,0},{29,1},{30,2},{31,3},{0,4},{1,5},{2,6},{3,7},{4,8},{5,9},{6... | collective-permute-start | bytes 195080 | tf_op jit(solution)/shard_map/ppermute | solution.py:32
  40.2 9.5 %collective-permute-start.11 = (f32[8,2,2,508]{3,2,1,0:T(2,128)S(1)}, f32[8,2,2,508]{3,2,1,0:T(2,128)S(1)}, u32[]{:S(2)}, u32[]{:S(2)}) collective-permute-start(f32[8,2,2,508]{3,2,1,0:T(2,128)S(1)} %broadcast_select_fusion.10), channel_id=1, source_target_pairs={{24,0},{25,1},{26,2},{27,3},{28,4},{29,5},{30,6},{31,7},{0,8},{1,9... | collective-permute-start | bytes 195080 | tf_op jit(solution)/shard_map/ppermute | solution.py:32
  44.3 9.8 %collective-permute-start.4 = (f32[8,2,2,508]{3,2,1,0:T(2,128)S(1)}, f32[8,2,2,508]{3,2,1,0:T(2,128)S(1)}, u32[]{:S(2)}, u32[]{:S(2)}) collective-permute-start(f32[8,2,2,508]{3,2,1,0:T(2,128)S(1)} %broadcast_select_fusion.20), channel_id=1, source_target_pairs={{24,0},{25,1},{26,2},{27,3},{28,4},{29,5},{30,6},{31,7},{0,8},{1,9... | collective-permute-start | bytes 195080 | tf_op jit(solution)/shard_map/ppermute | solution.py:32
  49.8 8.3 %collective-permute-start.12 = (f32[8,2,2,508]{3,2,1,0:T(2,128)S(1)}, f32[8,2,2,508]{3,2,1,0:T(2,128)S(1)}, u32[]{:S(2)}, u32[]{:S(2)}) collective-permute-start(f32[8,2,2,508]{3,2,1,0:T(2,128)S(1)} %broadcast_select_fusion.12), channel_id=1, source_target_pairs={{16,0},{17,1},{18,2},{19,3},{20,4},{21,5},{22,6},{23,7},{24,8},{25... | collective-permute-start | bytes 195080 | tf_op jit(solution)/shard_map/ppermute | solution.py:32
  54.2 16.9 %collective-permute-start.5 = (f32[8,2,2,508]{3,2,1,0:T(2,128)S(1)}, f32[8,2,2,508]{3,2,1,0:T(2,128)S(1)}, u32[]{:S(2)}, u32[]{:S(2)}) collective-permute-start(f32[8,2,2,508]{3,2,1,0:T(2,128)S(1)} %broadcast_select_fusion.22), channel_id=1, source_target_pairs={{16,0},{17,1},{18,2},{19,3},{20,4},{21,5},{22,6},{23,7},{24,8},{25... | collective-permute-start | bytes 195080 | tf_op jit(solution)/shard_map/ppermute | solution.py:32
  58.1 17.3 %collective-permute-start.13 = (f32[8,2,2,508]{3,2,1,0:T(2,128)S(1)}, f32[8,2,2,508]{3,2,1,0:T(2,128)S(1)}, u32[]{:S(2)}, u32[]{:S(2)}) collective-permute-start(f32[8,2,2,508]{3,2,1,0:T(2,128)S(1)} %broadcast_select_fusion.14), channel_id=1, source_target_pairs={{31,0},{0,1},{1,2},{2,3},{3,4},{4,5},{5,6},{6,7},{7,8},{8,9},{9,10... | collective-permute-start | bytes 195080 | tf_op jit(solution)/shard_map/ppermute | solution.py:32
  71.1 5.6 %collective-permute-start.6 = (f32[8,2,2,508]{3,2,1,0:T(2,128)S(1)}, f32[8,2,2,508]{3,2,1,0:T(2,128)S(1)}, u32[]{:S(2)}, u32[]{:S(2)}) collective-permute-start(f32[8,2,2,508]{3,2,1,0:T(2,128)S(1)} %broadcast_select_fusion.24), channel_id=1, source_target_pairs={{31,0},{0,1},{1,2},{2,3},{3,4},{4,5},{5,6},{6,7},{7,8},{8,9},{9,10... | collective-permute-start | bytes 195080 | tf_op jit(solution)/shard_map/ppermute | solution.py:32
  75.6 1.3 copy-start
  77.1 9.8 %collective-permute-start.15 = (f32[8,2,8,2]{3,2,1,0:T(8,128)S(1)}, f32[8,2,8,2]{3,2,1,0:T(8,128)S(1)}, u32[]{:S(2)}, u32[]{:S(2)}) collective-permute-start(f32[8,2,8,2]{3,2,1,0:T(8,128)S(1)} %get-tuple-element.174), channel_id=1, source_target_pairs={{1,0},{2,1},{3,2},{4,3},{5,4},{6,5},{7,6},{8,7},{9,8},{10,9},{11,1... | collective-permute-start | bytes 3080 | tf_op jit(solution)/shard_map/ppermute | solution.py:24
  79.0 9.2 %collective-permute-start.14 = (f32[8,2,8,2]{3,2,1,0:T(8,128)S(1)}, f32[8,2,8,2]{3,2,1,0:T(8,128)S(1)}, u32[]{:S(2)}, u32[]{:S(2)}) collective-permute-start(f32[8,2,8,2]{3,2,1,0:T(8,128)S(1)} %get-tuple-element.173), channel_id=1, source_target_pairs={{0,1},{1,2},{2,3},{3,4},{4,5},{5,6},{6,7},{7,8},{8,9},{9,10},{10,1... | collective-permute-start | bytes 3080 | tf_op jit(solution)/shard_map/ppermute | solution.py:23
  92.7 5.4 %collective-permute-start.23 = (f32[8,2,2,508]{3,2,1,0:T(2,128)S(1)}, f32[8,2,2,508]{3,2,1,0:T(2,128)S(1)}, u32[]{:S(2)}, u32[]{:S(2)}) collective-permute-start(f32[8,2,2,508]{3,2,1,0:T(2,128)S(1)} %get-tuple-element.184), channel_id=1, source_target_pairs={{32,0},{64,32},{96,64},{128,96},{160,128},{192,160},{224,192},{256... | collective-permute-start | bytes 195080 | tf_op jit(solution)/shard_map/ppermute | solution.py:24
  96.2 10.7 %collective-permute-start.16 = (f32[8,2,2,508]{3,2,1,0:T(2,128)S(1)}, f32[8,2,2,508]{3,2,1,0:T(2,128)S(1)}, u32[]{:S(2)}, u32[]{:S(2)}) collective-permute-start(f32[8,2,2,508]{3,2,1,0:T(2,128)S(1)} %get-tuple-element.183), channel_id=1, source_target_pairs={{0,32},{32,64},{64,96},{96,128},{128,160},{160,192},{192,224},{224... | collective-permute-start | bytes 195080 | tf_op jit(solution)/shard_map/ppermute | solution.py:23
  98.1 15.1 %collective-permute-start.24 = (f32[8,2,2,508]{3,2,1,0:T(2,128)S(1)}, f32[8,2,2,508]{3,2,1,0:T(2,128)S(1)}, u32[]{:S(2)}, u32[]{:S(2)}) collective-permute-start(f32[8,2,2,508]{3,2,1,0:T(2,128)S(1)} %collective-permute-done.23), channel_id=1, source_target_pairs={{31,0},{0,1},{1,2},{2,3},{3,4},{4,5},{5,6},{6,7},{7,8},{8,9},{9,10... | collective-permute-start | bytes 195080 | tf_op jit(solution)/shard_map/ppermute | solution.py:32
  106.9 8.3 %collective-permute-start.17 = (f32[8,2,2,508]{3,2,1,0:T(2,128)S(1)}, f32[8,2,2,508]{3,2,1,0:T(2,128)S(1)}, u32[]{:S(2)}, u32[]{:S(2)}) collective-permute-start(f32[8,2,2,508]{3,2,1,0:T(2,128)S(1)} %collective-permute-done.16), channel_id=1, source_target_pairs={{31,0},{0,1},{1,2},{2,3},{3,4},{4,5},{5,6},{6,7},{7,8},{8,9},{9,10... | collective-permute-start | bytes 195080 | tf_op jit(solution)/shard_map/ppermute | solution.py:32
  113.3 5.0 %collective-permute-start.25 = (f32[8,2,2,508]{3,2,1,0:T(2,128)S(1)}, f32[8,2,2,508]{3,2,1,0:T(2,128)S(1)}, u32[]{:S(2)}, u32[]{:S(2)}) collective-permute-start(f32[8,2,2,508]{3,2,1,0:T(2,128)S(1)} %broadcast_select_fusion.5), channel_id=1, source_target_pairs={{30,0},{31,1},{0,2},{1,3},{2,4},{3,5},{4,6},{5,7},{6,8},{7,9},{8,1... | collective-permute-start | bytes 195080 | tf_op jit(solution)/shard_map/ppermute | solution.py:32
  115.2 5.0 %collective-permute-start.18 = (f32[8,2,2,508]{3,2,1,0:T(2,128)S(1)}, f32[8,2,2,508]{3,2,1,0:T(2,128)S(1)}, u32[]{:S(2)}, u32[]{:S(2)}) collective-permute-start(f32[8,2,2,508]{3,2,1,0:T(2,128)S(1)} %broadcast_select_fusion.15), channel_id=1, source_target_pairs={{30,0},{31,1},{0,2},{1,3},{2,4},{3,5},{4,6},{5,7},{6,8},{7,9},{8,1... | collective-permute-start | bytes 195080 | tf_op jit(solution)/shard_map/ppermute | solution.py:32
  118.3 6.6 %collective-permute-start.26 = (f32[8,2,2,508]{3,2,1,0:T(2,128)S(1)}, f32[8,2,2,508]{3,2,1,0:T(2,128)S(1)}, u32[]{:S(2)}, u32[]{:S(2)}) collective-permute-start(f32[8,2,2,508]{3,2,1,0:T(2,128)S(1)} %broadcast_select_fusion.7), channel_id=1, source_target_pairs={{28,0},{29,1},{30,2},{31,3},{0,4},{1,5},{2,6},{3,7},{4,8},{5,9},{6... | collective-permute-start | bytes 195080 | tf_op jit(solution)/shard_map/ppermute | solution.py:32
  120.3 10.5 %collective-permute-start.19 = (f32[8,2,2,508]{3,2,1,0:T(2,128)S(1)}, f32[8,2,2,508]{3,2,1,0:T(2,128)S(1)}, u32[]{:S(2)}, u32[]{:S(2)}) collective-permute-start(f32[8,2,2,508]{3,2,1,0:T(2,128)S(1)} %broadcast_select_fusion.17), channel_id=1, source_target_pairs={{28,0},{29,1},{30,2},{31,3},{0,4},{1,5},{2,6},{3,7},{4,8},{5,9},{6... | collective-permute-start | bytes 195080 | tf_op jit(solution)/shard_map/ppermute | solution.py:32
  125.0 10.3 %collective-permute-start.27 = (f32[8,2,2,508]{3,2,1,0:T(2,128)S(1)}, f32[8,2,2,508]{3,2,1,0:T(2,128)S(1)}, u32[]{:S(2)}, u32[]{:S(2)}) collective-permute-start(f32[8,2,2,508]{3,2,1,0:T(2,128)S(1)} %broadcast_select_fusion.9), channel_id=1, source_target_pairs={{24,0},{25,1},{26,2},{27,3},{28,4},{29,5},{30,6},{31,7},{0,8},{1,9... | collective-permute-start | bytes 195080 | tf_op jit(solution)/shard_map/ppermute | solution.py:32
  130.8 9.4 %collective-permute-start.20 = (f32[8,2,2,508]{3,2,1,0:T(2,128)S(1)}, f32[8,2,2,508]{3,2,1,0:T(2,128)S(1)}, u32[]{:S(2)}, u32[]{:S(2)}) collective-permute-start(f32[8,2,2,508]{3,2,1,0:T(2,128)S(1)} %broadcast_select_fusion.19), channel_id=1, source_target_pairs={{24,0},{25,1},{26,2},{27,3},{28,4},{29,5},{30,6},{31,7},{0,8},{1,9... | collective-permute-start | bytes 195080 | tf_op jit(solution)/shard_map/ppermute | solution.py:32
  135.3 8.2 %collective-permute-start.28 = (f32[8,2,2,508]{3,2,1,0:T(2,128)S(1)}, f32[8,2,2,508]{3,2,1,0:T(2,128)S(1)}, u32[]{:S(2)}, u32[]{:S(2)}) collective-permute-start(f32[8,2,2,508]{3,2,1,0:T(2,128)S(1)} %broadcast_select_fusion.11), channel_id=1, source_target_pairs={{16,0},{17,1},{18,2},{19,3},{20,4},{21,5},{22,6},{23,7},{24,8},{25... | collective-permute-start | bytes 195080 | tf_op jit(solution)/shard_map/ppermute | solution.py:32
  140.3 18.7 %collective-permute-start.21 = (f32[8,2,2,508]{3,2,1,0:T(2,128)S(1)}, f32[8,2,2,508]{3,2,1,0:T(2,128)S(1)}, u32[]{:S(2)}, u32[]{:S(2)}) collective-permute-start(f32[8,2,2,508]{3,2,1,0:T(2,128)S(1)} %broadcast_select_fusion.21), channel_id=1, source_target_pairs={{16,0},{17,1},{18,2},{19,3},{20,4},{21,5},{22,6},{23,7},{24,8},{25... | collective-permute-start | bytes 195080 | tf_op jit(solution)/shard_map/ppermute | solution.py:32
  143.5 19.7 %collective-permute-start.29 = (f32[8,2,2,508]{3,2,1,0:T(2,128)S(1)}, f32[8,2,2,508]{3,2,1,0:T(2,128)S(1)}, u32[]{:S(2)}, u32[]{:S(2)}) collective-permute-start(f32[8,2,2,508]{3,2,1,0:T(2,128)S(1)} %broadcast_select_fusion.13), channel_id=1, source_target_pairs={{31,0},{0,1},{1,2},{2,3},{3,4},{4,5},{5,6},{6,7},{7,8},{8,9},{9,10... | collective-permute-start | bytes 195080 | tf_op jit(solution)/shard_map/ppermute | solution.py:32
  159.0 5.5 %collective-permute-start.22 = (f32[8,2,2,508]{3,2,1,0:T(2,128)S(1)}, f32[8,2,2,508]{3,2,1,0:T(2,128)S(1)}, u32[]{:S(2)}, u32[]{:S(2)}) collective-permute-start(f32[8,2,2,508]{3,2,1,0:T(2,128)S(1)} %broadcast_select_fusion.23), channel_id=1, source_target_pairs={{31,0},{0,1},{1,2},{2,3},{3,4},{4,5},{5,6},{6,7},{7,8},{8,9},{9,10... | collective-permute-start | bytes 195080 | tf_op jit(solution)/shard_map/ppermute | solution.py:32
  164.9 9.8 %copy-start.1 = (s32[4]{0:T(128)S(1)}, s32[4]{0:T(128)}, u32[]{:S(2)}) copy-start(s32[4]{0:T(128)} %param.6) | copy-start | bytes 52
  164.9 9.9 %collective-permute-start.31 = (f32[8,2,8,2]{3,2,1,0:T(8,128)S(1)}, f32[8,2,8,2]{3,2,1,0:T(8,128)S(1)}, u32[]{:S(2)}, u32[]{:S(2)}) collective-permute-start(f32[8,2,8,2]{3,2,1,0:T(8,128)S(1)} %get-tuple-element.132), channel_id=1, source_target_pairs={{1,0},{2,1},{3,2},{4,3},{5,4},{6,5},{7,6},{8,7},{9,8},{10,9},{11,1... | collective-permute-start | bytes 3080 | tf_op jit(solution)/shard_map/ppermute | solution.py:24
  166.9 9.2 %collective-permute-start.30 = (f32[8,2,8,2]{3,2,1,0:T(8,128)S(1)}, f32[8,2,8,2]{3,2,1,0:T(8,128)S(1)}, u32[]{:S(2)}, u32[]{:S(2)}) collective-permute-start(f32[8,2,8,2]{3,2,1,0:T(8,128)S(1)} %get-tuple-element.131), channel_id=1, source_target_pairs={{0,1},{1,2},{2,3},{3,4},{4,5},{5,6},{6,7},{7,8},{8,9},{9,10},{10,1... | collective-permute-start | bytes 3080 | tf_op jit(solution)/shard_map/ppermute | solution.py:23
  180.8 9.8 %collective-permute-start.32 = (f32[8,2,4,508]{3,2,1,0:T(4,128)S(1)}, f32[8,2,4,508]{3,2,1,0:T(4,128)S(1)}, u32[]{:S(2)}, u32[]{:S(2)}) collective-permute-start(f32[8,2,4,508]{3,2,1,0:T(4,128)S(1)} %fusion.2), channel_id=1, source_target_pairs={{31,0},{0,1},{1,2},{2,3},{3,4},{4,5},{5,6},{6,7},{7,8},{8,9},{9,10... | collective-permute-start | bytes 390152 | tf_op jit(solution)/shard_map/ppermute | solution.py:32
  190.7 5.7 %collective-permute-start.33 = (f32[8,2,4,508]{3,2,1,0:T(4,128)S(1)}, f32[8,2,4,508]{3,2,1,0:T(4,128)S(1)}, u32[]{:S(2)}, u32[]{:S(2)}) collective-permute-start(f32[8,2,4,508]{3,2,1,0:T(4,128)S(1)} %broadcast_select_fusion), channel_id=1, source_target_pairs={{30,0},{31,1},{0,2},{1,3},{2,4},{3,5},{4,6},{5,7},{6,8},{7,9},{8,1... | collective-permute-start | bytes 390152 | tf_op jit(solution)/shard_map/ppermute | solution.py:32
  196.5 7.4 %collective-permute-start.34 = (f32[8,2,4,508]{3,2,1,0:T(4,128)S(1)}, f32[8,2,4,508]{3,2,1,0:T(4,128)S(1)}, u32[]{:S(2)}, u32[]{:S(2)}) collective-permute-start(f32[8,2,4,508]{3,2,1,0:T(4,128)S(1)} %broadcast_select_fusion.1), channel_id=1, source_target_pairs={{28,0},{29,1},{30,2},{31,3},{0,4},{1,5},{2,6},{3,7},{4,8},{5,9},{6... | collective-permute-start | bytes 390152 | tf_op jit(solution)/shard_map/ppermute | solution.py:32
  204.0 9.6 %collective-permute-start.35 = (f32[8,2,4,508]{3,2,1,0:T(4,128)S(1)}, f32[8,2,4,508]{3,2,1,0:T(4,128)S(1)}, u32[]{:S(2)}, u32[]{:S(2)}) collective-permute-start(f32[8,2,4,508]{3,2,1,0:T(4,128)S(1)} %broadcast_select_fusion.2), channel_id=1, source_target_pairs={{24,0},{25,1},{26,2},{27,3},{28,4},{29,5},{30,6},{31,7},{0,8},{1,9... | collective-permute-start | bytes 390152 | tf_op jit(solution)/shard_map/ppermute | solution.py:32
  213.7 3.4 %copy-start.2 = (s32[4]{0:T(128)S(1)}, s32[4]{0:T(128)}, u32[]{:S(2)}) copy-start(s32[4]{0:T(128)} %param.7) | copy-start | bytes 52
  213.8 7.2 %collective-permute-start.36 = (f32[8,2,4,508]{3,2,1,0:T(4,128)S(1)}, f32[8,2,4,508]{3,2,1,0:T(4,128)S(1)}, u32[]{:S(2)}, u32[]{:S(2)}) collective-permute-start(f32[8,2,4,508]{3,2,1,0:T(4,128)S(1)} %broadcast_select_fusion.3), channel_id=1, source_target_pairs={{16,0},{17,1},{18,2},{19,3},{20,4},{21,5},{22,6},{23,7},{24,8},{25... | collective-permute-start | bytes 390152 | tf_op jit(solution)/shard_map/ppermute | solution.py:32
  221.1 30.7 %collective-permute-start.37 = (f32[8,2,4,508]{3,2,1,0:T(4,128)S(1)}, f32[8,2,4,508]{3,2,1,0:T(4,128)S(1)}, u32[]{:S(2)}, u32[]{:S(2)}) collective-permute-start(f32[8,2,4,508]{3,2,1,0:T(4,128)S(1)} %broadcast_select_fusion.4), channel_id=1, source_target_pairs={{31,0},{0,1},{1,2},{2,3},{3,4},{4,5},{5,6},{6,7},{7,8},{8,9},{9,10... | collective-permute-start | bytes 390152 | tf_op jit(solution)/shard_map/ppermute | solution.py:32
where the time goes:
time: 258 us; the launch traced here: 256 us
  starting transfers between devices  196 us (76%)
  waiting for transfers between devices  32.5 us (13%)
  other arithmetic  10.6 us (4%)
  between operations  10.1 us (4%)
  local copies, waits for them, and re-layouts  7.11 us (3%)
    ppermute x30, starting transfers between devices, shifted_2(): return lax.ppermute(block, axis, route)  158 us
    ppermute x30, waiting for transfers between devices, shifted_2(): return lax.ppermute(block, axis, route)  29.9 us
    ppermute x4, starting transfers between devices, with_halo(): before = lax.ppermute(last, axis, up)  19.6 us
    ppermute x4, starting transfers between devices, with_halo(): after = lax.ppermute(leading, axis, down)  18.9 us
  transfers between devices with their start and end apart: 38, of which 13 were waited for; matrix products, arithmetic and copies ran while one was open for 1% of the time, Pallas kernels for 0%

commit v1 on v0

v1 whole, which is shorter than its diff:
```python
import functools

import jax
import jax.numpy as jnp
from jax import lax
from jax.experimental import pallas as pl
from jax.experimental.pallas import tpu as pltpu
from jax.sharding import PartitionSpec as P

FRAC = 16
GAMMA_LESS = 5.0 / 3.0 - 1.0
ROTATION = 1.0
SHEAR_RATE = 1.5
MAX_SPEED = 5.0
TIME_STEP = 0.05

FACE_X, FACE_Y, FACE_Z, NEXT_Y = 5, 6, 7, 8
ROWS = 4
LINES = 8 * ROWS
STRIPS = 17
MESH = pl.DeviceIdType.MESH


def ahead(value, count):
    lane = lax.broadcasted_iota(jnp.int32, value.shape, 2)
    moved = pltpu.roll(value, 128 - count, 2)
    return jnp.where(lane >= 128 - count, pltpu.roll(moved, 7, 1), moved)


def behind(value, count):
    lane = lax.broadcasted_iota(jnp.int32, value.shape, 2)
    moved = pltpu.roll(value, count, 2)
    return jnp.where(lane < count, pltpu.roll(moved, 1, 1), moved)


def other_plane(value):
    return pltpu.roll(value, 4, 1)


def euler(fields, next_y):
    density, mom_x, mom_y, mom_z, energy, face_x, face_y, face_z = fields
    rows = density.shape[0]
    mid = slice(1, rows - 1)
    cen_x = 0.5 * (face_x[:-1] + face_x[1:])
    cen_y = 0.5 * (face_y + next_y)
    cen_z = 0.5 * (face_z + other_plane(face_z))
    inverse = 1.0 / density
    vel_x = mom_x * inverse
    vel_y = mom_y * inverse
    vel_z = mom_z * inverse
    magnetic = 0.5 * (cen_x * cen_x + cen_y * cen_y + cen_z * cen_z)
    pressure = (
        GAMMA_LESS * (energy - 0.5 * (mom_x * vel_x + mom_y * vel_y + mom_z * vel_z) - magnetic) + magnetic
    )
    vel_dot = vel_x * cen_x + vel_y * cen_y + vel_z * cen_z
    conserved = (density, mom_x, mom_y, mom_z, energy)
    momenta = (mom_x, mom_y, mom_z)
    centred = (cen_x, cen_y, cen_z)
    velocity = (vel_x, vel_y, vel_z)
    change = [None] * 5
    for normal in range(3):
        part = slice(None) if normal == 0 else mid
        speed = velocity[normal][part]
        across = centred[normal][part]
        fluxes = [momenta[normal][part]]
        for second in range(3):
            term = momenta[second][part] * speed - across * centred[second][part]
            if second == normal:
                term = term + pressure[part]
            fluxes.append(term)
        fluxes.append((energy[part] + pressure[part]) * speed - across * vel_dot[part])
        for member in range(5):
            flux = fluxes[member]
            held = conserved[member][part]
            if normal == 0:
                upwind = 0.5 * (flux[:-1] + flux[1:]) - 0.5 * MAX_SPEED * (held[1:] - held[:-1])
                delta = upwind[1:] - upwind[:-1]
            elif normal == 1:
                upwind = 0.5 * (behind(flux, 1) + flux) - 0.5 * MAX_SPEED * (held - behind(held, 1))
                delta = ahead(upwind, 1) - upwind
            else:
                upwind = 0.5 * (other_plane(flux) + flux) - 0.5 * MAX_SPEED * (held - other_plane(held))
                delta = other_plane(upwind) - upwind
            change[member] = -delta if change[member] is None else change[member] - delta
    change[1] = change[1] + 2.0 * ROTATION * mom_y[mid]
    change[2] = change[2] - (2.0 - SHEAR_RATE) * ROTATION * mom_x[mid]
    change[4] = change[4] + SHEAR_RATE * ROTATION * (mom_x[mid] * vel_y[mid] - cen_x[mid] * cen_y[mid])
    elec_x = -(vel_y * cen_z - vel_z * cen_y)
    elec_y = -(vel_z * cen_x - vel_x * cen_z)
    elec_z = -(vel_x * cen_y - vel_y * cen_x)
    pair_x = elec_x[mid] + behind(elec_x[mid], 1)
    edge_x = 0.25 * (pair_x + other_plane(pair_x))
    pair_y = elec_y[1:] + elec_y[:-1]
    edge_y = 0.25 * (pair_y + other_plane(pair_y))
    pair_z = elec_z[1:] + elec_z[:-1]
    edge_z = 0.25 * (pair_z + behind(pair_z, 1))
    delta_x = -(ahead(edge_z, 1) - edge_z - (other_plane(edge_y) - edge_y))
    delta_y = -(other_plane(edge_x) - edge_x - (edge_z[1:] - edge_z[:-1]))
    delta_z = -(edge_y[1:] - edge_y[:-1] - (ahead(edge_x, 1) - edge_x))
    done = [conserved[member][mid] + TIME_STEP * change[member] for member in range(5)]
    done.append(face_x[1:rows] + TIME_STEP * delta_x)
    done.append(face_y[mid] + TIME_STEP * delta_y)
    done.append(face_z[mid] + TIME_STEP * delta_z)
    return done


def window(ref, slot, blocks, cells, amount, kinds):
    hops = lax.div(amount, cells)
    rest = lax.rem(amount, cells)
    if kinds == 3:
        low = rest < 2
        hops = jnp.where(low, hops - 1, hops)
        rest = jnp.where(low, rest + cells, rest)
    total = blocks * 8
    lane = lax.broadcasted_iota(jnp.int32, (blocks, 8, 128), 2)
    chunk = lax.broadcasted_iota(jnp.int32, (blocks, 8, 128), 1) % 4
    place = chunk * 128 + lane - 2 - rest
    result = None
    for kind in reversed(range(kinds)):
        distance = rest - kind * cells + 1024
        lanes = lax.rem(distance, 128)
        sublanes = lax.div(distance, 128) - 8
        back = lax.rem(8 * (hops + kind) + sublanes + total, total)
        near = ref[slot, pl.ds(total - back, total), :].reshape(blocks, 8, 128)
        far = ref[slot, pl.ds(total - back - 1, total), :].reshape(blocks, 8, 128)
        near = pltpu.roll(near, lanes, 2)
        far = pltpu.roll(far, lanes, 2)
        moved = jnp.where(lane >= lanes, near, far)
        if result is None:
            result = moved
        else:
            result = jnp.where(place >= -kind * cells, moved, result)
    return result


def kernel(
    n_gx,
    n_gy,
    cells,
    shear_ref,
    remap_ref,
    frac_ref,
    state_ref,
    out_ref,
    raw,
    held,
    ext,
    last_face,
    to_left,
    to_right,
    from_left,
    from_right,
    edges,
    next_edges,
    strip_in,
    strip_out,
    moved,
    line_in,
    line_out,
    lines,
    send_sems,
    recv_sems,
):
    gx = lax.axis_index("gx")
    gy = lax.axis_index("gy")
    half = n_gy // 2
    slots = -(-STRIPS // n_gy)
    per = LINES // n_gy
    left_y = lax.rem(gy + n_gy - 1, n_gy)
    right_y = lax.rem(gy + 1, n_gy)
    first_x = gx == 0
    last_x = gx == n_gx - 1
    edge_x = jnp.logical_or(first_x, last_x)
    facing = jnp.where(first_x, n_gx - 1, 0)
    barrier = pltpu.get_barrier_semaphore()

    def greet(x, y):
        pl.semaphore_signal(barrier, inc=1, device_id=(x, y), device_id_type=MESH)

    def send(source, target, sem, x, y):
        return pltpu.make_async_remote_copy(
            src_ref=source,
            dst_ref=target,
            send_sem=send_sems.at[sem],
            recv_sem=recv_sems.at[sem],
            device_id=(x, y),
            device_id_type=MESH,
        )

    def wait_bytes(ref, sem):
        pltpu.make_async_copy(ref, ref, sem).wait()

    def peers(body):
        def step(k, carry):
            body(lax.rem(gy + k, n_gy))
            return carry

        lax.fori_loop(1, n_gy, step, 0)

    peers(lambda y: greet(gx, y))

    @pl.when(jnp.logical_not(first_x))
    def _():
        greet(gx - 1, gy)

    @pl.when(jnp.logical_not(last_x))
    def _():
        greet(gx + 1, gy)

    @pl.when(edge_x)
    def _():
        def step(y, carry):
            greet(facing, y)
            return carry

        lax.fori_loop(0, n_gy, step, 0)

    whole = cells // 128
    for field in range(8):
        for plane in range(2):
            for chunk in range(4):
                if chunk < whole:
                    part = state_ref[field, plane, :, pl.ds(128 * chunk, 128)]
                else:
                    part = state_ref[field, plane, :, pl.ds(128 * whole, cells - 128 * whole)]
                    part = jnp.concatenate([part, jnp.zeros((ROWS, 128 * (whole + 1) - cells), jnp.float32)], axis=1)
                raw[pl.ds(field * 32 + plane * 4 + chunk, ROWS, stride=8), :] = part
    to_left[...] = raw[pl.ds(0, 64, stride=4), :]
    to_right[...] = raw[pl.ds(3, 64, stride=4), :]
    held[...] = behind(raw[...].reshape(LINES, 8, 128), 2)
    pl.semaphore_wait(barrier, n_gy - 1 + jnp.where(edge_x, n_gy + 1, 2))

    strip_left = send(to_left, from_right, 0, gx, left_y)
    strip_right = send(to_right, from_left, 1, gx, right_y)
    strip_left.start()
    strip_right.start()
    base = jnp.where(first_x, 0, 2)

    def boundary_tile(t):
        plain = lax.div(t, 2) * ROWS + base + lax.rem(t, 2)
        return jnp.where(t == STRIPS - 1, FACE_X * ROWS + 2, plain)

    mine = jnp.where(lax.rem(gy, 2) == 0, lax.div(gy, 2), half + lax.div(gy, 2))

    @pl.when(edge_x)
    def _():
        def step(t, carry):
            rank = lax.rem(t, n_gy)
            slot = lax.div(t, n_gy)
            owner = jnp.where(rank < half, 2 * rank, 2 * (rank - half) + 1)
            source = held.at[boundary_tile(t)]
            target = strip_in.at[slot, pl.ds(pl.multiple_of(8 * gy, 8), 8), :]

            @pl.when(owner != gy)
            def _():
                send(source, target, 2, gx, owner).start()

            @pl.when(owner == gy)
            def _():
                pltpu.make_async_copy(source, target, recv_sems.at[2]).start()

            return carry

        lax.fori_loop(0, STRIPS, step, 0)

    strip_left.wait_recv()
    strip_right.wait_recv()
    lane = lax.broadcasted_iota(jnp.int32, (LINES, 8, 128), 2)
    chunk = lax.broadcasted_iota(jnp.int32, (LINES, 8, 128), 1) % 4
    beyond = cells % 128
    after = from_right[...]
    edges[pl.ds(0, 64, stride=4), :] = pltpu.roll(from_left[...], 130 - beyond, 1)
    edges[pl.ds(3, 64, stride=4), :] = pltpu.roll(after, beyond + 2, 1)
    outside = jnp.logical_or(
        jnp.logical_and(chunk == 0, lane < 2), jnp.logical_and(chunk == 3, lane >= beyond + 2)
    )
    full = jnp.where(outside, edges[...].reshape(LINES, 8, 128), held[...])
    for field in range(8):
        ext[field, 2:6] = full[ROWS * field : ROWS * field + ROWS]
    next_edges[pl.ds(3, 2 * ROWS, stride=4), :] = pltpu.roll(after[2 * ROWS * FACE_Y : 2 * ROWS * (FACE_Y + 1)], beyond + 1, 1)
    final = jnp.logical_and(chunk == 3, lane == 127)[:ROWS]
    ext[NEXT_Y, 2:6] = jnp.where(
        final, next_edges[...].reshape(ROWS, 8, 128), ahead(full[ROWS * FACE_Y : ROWS * (FACE_Y + 1)], 1)
    )

    to_up = send(ext.at[:, pl.ds(4, 2)], ext.at[:, pl.ds(0, 2)], 3, gx + 1, gy)
    to_down = send(ext.at[:, pl.ds(2, 2)], ext.at[:, pl.ds(6, 2)], 4, gx - 1, gy)
    to_down_face = send(ext.at[FACE_X, 4], last_face, 5, gx - 1, gy)

    @pl.when(jnp.logical_not(last_x))
    def _():
        to_up.start()

    @pl.when(jnp.logical_not(first_x))
    def _():
        to_down.start()
        to_down_face.start()

    @pl.when(edge_x)
    def _():
        total_cells = cells * n_gy
        offset = shear_ref[0]
        amount = jnp.where(first_x, lax.rem(total_cells - offset, total_cells), offset)
        amount_next = lax.rem(amount + total_cells - 1, total_cells)
        landing = jnp.where(first_x, 6, 0)

        def ship(tiles, field, row, sem):
            def step(y, carry):
                send(tiles.at[y], ext.at[field, row], sem, facing, y).start()
                return carry

            lax.fori_loop(0, n_gy, step, 0)

        def ship_face(tiles):
            def step(y, carry):
                send(tiles.at[y], last_face, 5, facing, y).start()
                return carry

            lax.fori_loop(0, n_gy, step, 0)

        for slot in range(slots):
            t = slot * n_gy + mine
            field = lax.div(t, 2)

            @pl.when(t < STRIPS)
            def _(slot=slot, t=t, field=field):
                block = strip_in.at[slot, pl.ds(0, 8 * n_gy), :]
                wait_bytes(block, recv_sems.at[2])
                strip_in[slot, pl.ds(8 * n_gy, 8 * n_gy), :] = strip_in[slot, pl.ds(0, 8 * n_gy), :]
                strip_out[slot] = window(strip_in, slot, n_gy, cells, amount, 3)

                @pl.when(t < STRIPS - 1)
                def _():
                    ship(strip_out.at[slot], field, landing + lax.rem(t, 2), jnp.where(first_x, 4, 3))

                @pl.when(jnp.logical_and(t == STRIPS - 1, first_x))
                def _():
                    ship_face(strip_out.at[slot])

                @pl.when(field == FACE_Y)
                def _():
                    moved[slot] = window(strip_in, slot, n_gy, cells, amount_next, 3)
                    ship(moved.at[slot], NEXT_Y, landing + lax.rem(t, 2), jnp.where(first_x, 4, 3))

    wait_bytes(ext.at[:, pl.ds(0, 2)], recv_sems.at[3])
    wait_bytes(ext.at[:, pl.ds(6, 2)], recv_sems.at[4])
    wait_bytes(last_face, recv_sems.at[5])

    fields = [ext[field] for field in range(8)]
    fields[FACE_X] = jnp.concatenate([fields[FACE_X], last_face[...][None]], axis=0)
    once = euler(fields, ext[NEXT_Y])
    twice = euler(once, ahead(once[FACE_Y], 1))
    for field in range(8):
        lines[ROWS * field : ROWS * field + ROWS] = 0.5 * (ext[field, 2:6] + twice[field][:ROWS])

    def spread(source, target, sem):
        def step(t, carry):
            owner = lax.div(t, per)

            @pl.when(owner != gy)
            def _():
                send(source(t, owner), target(t), sem, gx, owner).start()

            @pl.when(owner == gy)
            def _():
                pltpu.make_async_copy(source(t, owner), target(t), recv_sems.at[sem]).start()

            return carry

        lax.fori_loop(0, LINES, step, 0)

    spread(
        lambda t, owner: lines.at[t],
        lambda t: line_in.at[lax.rem(t, per), pl.ds(pl.multiple_of(8 * gy, 8), 8), :],
        6,
    )
    wait_bytes(line_in.at[:, pl.ds(0, 8 * n_gy), :], recv_sems.at[6])

    for slot in range(per):
        row = lax.rem(gy * per + slot, ROWS)
        line_in[slot, pl.ds(8 * n_gy, 8 * n_gy), :] = line_in[slot, pl.ds(0, 8 * n_gy), :]
        tiles = window(line_in, slot, n_gy, cells, remap_ref[row], 2)
        weight = (frac_ref[row].astype(jnp.float32) + 0.5) / FRAC
        line_out[slot] = (1.0 - weight) * ahead(tiles, 2) + weight * ahead(tiles, 1)

    def back(k, carry):
        y = lax.div(k, per)
        slot = lax.rem(k, per)
        source = line_out.at[slot, y]
        target = raw.at[pl.ds(pl.multiple_of(8 * (gy * per + slot), 8), 8), :]

        @pl.when(y != gy)
        def _():
            send(source, target, 7, gx, y).start()

        @pl.when(y == gy)
        def _():
            pltpu.make_async_copy(source, target, recv_sems.at[7]).start()

        return carry

    lax.fori_loop(0, LINES, back, 0)
    wait_bytes(raw, recv_sems.at[7])
    for field in range(8):
        for plane in range(2):
            for chunk in range(4):
                part = raw[pl.ds(field * 32 + plane * 4 + chunk, ROWS, stride=8), :]
                width = min(128, cells - 128 * chunk)
                out_ref[field, plane, :, pl.ds(128 * chunk, width)] = part[:, :width]

    strip_left.wait_send()
    strip_right.wait_send()

    @pl.when(jnp.logical_not(last_x))
    def _():
        to_up.wait_send()

    @pl.when(jnp.logical_not(first_x))
    def _():
        to_down.wait_send()
        to_down_face.wait_send()

    @pl.when(edge_x)
    def _():
        for count in range(STRIPS - slots, STRIPS + 1):
            own = sum((slot * n_gy + mine < STRIPS).astype(jnp.int32) for slot in range(slots))

            @pl.when(STRIPS - own == count)
            def _(count=count):
                wait_bytes(held.at[pl.ds(0, count)], send_sems.at[2])

        for slot in range(slots):
            t = slot * n_gy + mine
            field = lax.div(t, 2)

            @pl.when(t < STRIPS - 1)
            def _(slot=slot):
                wait_bytes(strip_out.at[slot], send_sems.at[jnp.where(first_x, 4, 3)])

            @pl.when(jnp.logical_and(t == STRIPS - 1, first_x))
            def _(slot=slot):
                wait_bytes(strip_out.at[slot], send_sems.at[5])

            @pl.when(jnp.logical_and(t < STRIPS, field == FACE_Y))
            def _(slot=slot):
                wait_bytes(moved.at[slot], send_sems.at[jnp.where(first_x, 4, 3)])

    wait_bytes(lines.at[pl.ds(0, LINES - per)], send_sems.at[6])
    wait_bytes(lines.at[pl.ds(0, LINES - per)], send_sems.at[7])


def solution(mesh):
    n_gx = mesh.shape["gx"]
    n_gy = mesh.shape["gy"]

    def shards(state, shear_offset, remap_shift, frac_index):
        cells = state.shape[3]
        per = LINES // n_gy
        slots = -(-STRIPS // n_gy)
        vmem = lambda *shape: pltpu.VMEM(shape, jnp.float32)
        small = pl.BlockSpec(memory_space=pltpu.SMEM)
        large = pl.BlockSpec(memory_space=pltpu.VMEM)
        return pl.pallas_call(
            functools.partial(kernel, n_gx, n_gy, cells),
            out_shape=jax.ShapeDtypeStruct(state.shape, jnp.float32),
            in_specs=[small, small, small, large],
            out_specs=large,
            scratch_shapes=[
                vmem(8 * LINES, 128),
                vmem(LINES, 8, 128),
                vmem(9, 8, 8, 128),
                vmem(8, 128),
                vmem(64, 128),
                vmem(64, 128),
                vmem(64, 128),
                vmem(64, 128),
                vmem(8 * LINES, 128),
                vmem(8 * ROWS, 128),
                vmem(slots, 16 * n_gy, 128),
                vmem(slots, n_gy, 8, 128),
                vmem(slots, n_gy, 8, 128),
                vmem(per, 16 * n_gy, 128),
                vmem(per, n_gy, 8, 128),
                vmem(LINES, 8, 128),
                pltpu.SemaphoreType.DMA((8,)),
                pltpu.SemaphoreType.DMA((8,)),
            ],
            compiler_params=pltpu.CompilerParams(collective_id=0, has_side_effects=True),
        )(shear_offset, remap_shift, frac_index, state)

    placed = (P(None, None, "gx", "gy"), P(), P("gx"), P("gx"))
    return jax.shard_map(shards, mesh=mesh, in_specs=placed, out_specs=P(None, None, "gx", "gy"), check_vma=False)
```

time: 258 us -> 50.2 us (0.19)
  the two profiles are of different devices: /device:TPU:57 before, /device:TPU:1 now
where the time goes in v1:
time: 50.2 us; the launch traced here: 50.1 us
  Pallas kernels  47.8 us (95%)
  local copies, waits for them, and re-layouts  1.57 us (3%)
  between operations  0.66 us (1%)
    pallas_call x1, Pallas kernels, shards(): pl.pallas_call(functools.partial(kernel, n_gx, n_gy, cells), out_shape=ja...  47.8 us
    unnamed x1, local copies, waits for them, and re-layouts  1.57 us

profile of v1, /device:TPU:1, one launch (start us, length us, event | category | flops | bytes accessed | tf_op | source)
XLA Modules:
  0.0 50.1 jit_solution(663632556814463435)
XLA Ops:
  0.7 47.8 %shard_map.46 = f32[8,2,4,508]{3,2,1,0:T(4,128)} custom-call(s32[1]{0:T(128)S(6)} %copy.6.shear_ref, s32[4]{0:T(128)} %remap_ref.1, s32[4]{0:T(128)} %frac_ref.1, f32[8,2,4,508]{3,2,1,0:T(4,128)} %state_ref.1), custom_call_target="tpu_custom_call" | custom-call | tf_op jit(solution)/shard_map/pallas_call | solution.py:463
  48.5 1.6 %copy.7 = f32[8,2,4,508]{3,2,1,0:T(4,128)} copy(f32[8,2,4,508]{3,2,1,0:T(4,128)} %shard_map.46) | data formatting | bytes 260096

commit v2 on v1

--- a/solution.py
+++ b/solution.py
@@ -137,11 +137,15 @@
     n_gx,
     n_gy,
     cells,
+    shear_hbm,
+    remap_hbm,
+    frac_hbm,
+    state_hbm,
+    out_ref,
     shear_ref,
     remap_ref,
     frac_ref,
     state_ref,
-    out_ref,
     raw,
     held,
     ext,
@@ -152,7 +156,8 @@
     from_right,
     edges,
     next_edges,
-    strip_in,
+    strip_in_0,
+    strip_in_1,
     strip_out,
     moved,
     line_in,
@@ -160,6 +165,8 @@
     lines,
     send_sems,
     recv_sems,
+    load_sems,
+    known,
 ):
     gx = lax.axis_index("gx")
     gy = lax.axis_index("gy")
@@ -168,21 +175,37 @@
     per = LINES // n_gy
     left_y = lax.rem(gy + n_gy - 1, n_gy)
     right_y = lax.rem(gy + 1, n_gy)
+    inside = lax.rem(gy, half)
+    side = gy - inside
+    core = gy + 1 - 2 * lax.rem(gy, 2)
+    up, down, up_2, down_2 = (side + lax.rem(inside + half + step, half) for step in (2, -2, 4, -4))
+    partner = lax.rem(gx + n_gx // 2, n_gx)
+    last = n_gx - 1
     first_x = gx == 0
-    last_x = gx == n_gx - 1
-    edge_x = jnp.logical_or(first_x, last_x)
-    facing = jnp.where(first_x, n_gx - 1, 0)
+    last_x = gx == last
+    strip_in = (strip_in_0, strip_in_1)
     barrier = pltpu.get_barrier_semaphore()
-
-    def greet(x, y):
-        pl.semaphore_signal(barrier, inc=1, device_id=(x, y), device_id_type=MESH)
-
-    def send(source, target, sem, x, y):
+    load = pltpu.make_async_copy(state_hbm, state_ref, load_sems.at[0])
+    load.start()
+    load_shear = pltpu.make_async_copy(shear_hbm, shear_ref, load_sems.at[1])
+    load_shear.start()
+
+    def tell(sem, x, y):
+        pl.semaphore_signal(sem, inc=1, device_id=(x, y), device_id_type=MESH)
+
+    def everyone(body):
+        def step(k, carry):
+            body(lax.rem(k + gy, n_gy))
+            return carry
+
+        lax.fori_loop(0, n_gy, step, 0)
+
+    def send(source, target, sent, arrived, x, y):
         return pltpu.make_async_remote_copy(
             src_ref=source,
             dst_ref=target,
-            send_sem=send_sems.at[sem],
-            recv_sem=recv_sems.at[sem],
+            send_sem=send_sems.at[sent],
+            recv_sem=recv_sems.at[arrived],
             device_id=(x, y),
             device_id_type=MESH,
         )
@@ -190,31 +213,25 @@
     def wait_bytes(ref, sem):
         pltpu.make_async_copy(ref, ref, sem).wait()
 
-    def peers(body):
-        def step(k, carry):
-            body(lax.rem(gy + k, n_gy))
-            return carry
-
-        lax.fori_loop(1, n_gy, step, 0)
-
-    peers(lambda y: greet(gx, y))
+    for y in (left_y, right_y, up, down):
+        tell(barrier, gx, y)
+    for y in (gy, lax.rem(gy + half, n_gy)):
+        tell(barrier, partner, y)
 
     @pl.when(jnp.logical_not(first_x))
     def _():
-        greet(gx - 1, gy)
+        tell(barrier, gx - 1, gy)
 
     @pl.when(jnp.logical_not(last_x))
     def _():
-        greet(gx + 1, gy)
-
-    @pl.when(edge_x)
-    def _():
-        def step(y, carry):
-            greet(facing, y)
-            return carry
-
-        lax.fori_loop(0, n_gy, step, 0)
-
+        tell(barrier, gx + 1, gy)
+
+    @pl.when(first_x)
+    def _():
+        tell(barrier, 0, lax.rem(gy + half, n_gy))
+        everyone(lambda y: tell(barrier, last, y))
+
+    load.wait()
     whole = cells // 128
     for field in range(8):
         for plane in range(2):
@@ -228,40 +245,62 @@
     to_left[...] = raw[pl.ds(0, 64, stride=4), :]
     to_right[...] = raw[pl.ds(3, 64, stride=4), :]
     held[...] = behind(raw[...].reshape(LINES, 8, 128), 2)
-    pl.semaphore_wait(barrier, n_gy - 1 + jnp.where(edge_x, n_gy + 1, 2))
-
-    strip_left = send(to_left, from_right, 0, gx, left_y)
-    strip_right = send(to_right, from_left, 1, gx, right_y)
-    strip_left.start()
-    strip_right.start()
-    base = jnp.where(first_x, 0, 2)
-
-    def boundary_tile(t):
-        plain = lax.div(t, 2) * ROWS + base + lax.rem(t, 2)
-        return jnp.where(t == STRIPS - 1, FACE_X * ROWS + 2, plain)
-
-    mine = jnp.where(lax.rem(gy, 2) == 0, lax.div(gy, 2), half + lax.div(gy, 2))
-
-    @pl.when(edge_x)
-    def _():
-        def step(t, carry):
+    pl.semaphore_wait(barrier, jnp.where(last_x, 7 + n_gy, 8))
+    for y in (core, up, down):
+        tell(known.at[0], gx, y)
+
+    def strips_to_first(count, base, way):
+        def step(k, carry):
+            t = lax.rem(k + lax.div(gy, 2), count)
             rank = lax.rem(t, n_gy)
             slot = lax.div(t, n_gy)
             owner = jnp.where(rank < half, 2 * rank, 2 * (rank - half) + 1)
-            source = held.at[boundary_tile(t)]
-            target = strip_in.at[slot, pl.ds(pl.multiple_of(8 * gy, 8), 8), :]
-
-            @pl.when(owner != gy)
+            tile = lax.div(t, 2) * ROWS + base + lax.rem(t, 2)
+            tile = jnp.where(t == STRIPS - 1, FACE_X * ROWS + 2, tile)
+            target = strip_in[way].at[slot, pl.ds(pl.multiple_of(8 * gy, 8), 8), :]
+            arrived = 8 + slots * way + slot
+
+            @pl.when(jnp.logical_or(last_x, owner != gy))
             def _():
-                send(source, target, 2, gx, owner).start()
-
-            @pl.when(owner == gy)
+                send(held.at[tile], target, 2, arrived, 0, owner).start()
+
+            @pl.when(jnp.logical_and(first_x, owner == gy))
             def _():
-                pltpu.make_async_copy(source, target, recv_sems.at[2]).start()
+                pltpu.make_async_copy(held.at[tile], target, recv_sems.at[arrived]).start()
 
             return carry
 
-        lax.fori_loop(0, STRIPS, step, 0)
+        lax.fori_loop(0, count, step, 0)
+
+    @pl.when(last_x)
+    def _():
+        strips_to_first(STRIPS - 1, 2, 1)
+        everyone(lambda y: tell(known.at[3], 0, y))
+
+    strip_left = send(to_left, from_right, 0, 0, gx, left_y)
+    strip_right = send(to_right, from_left, 1, 1, gx, right_y)
+    strip_left.start()
+    strip_right.start()
+    amounts = send(remap_hbm, remap_ref, 10, 8 + 2 * slots, partner, gy)
+    levels = send(frac_hbm, frac_ref, 11, 9 + 2 * slots, partner, gy)
+    amounts.start()
+    levels.start()
+    pl.semaphore_wait(known.at[0], 3)
+    if half > 4:
+        for y in (up_2, down_2):
+            tell(known.at[1], gx, y)
+        pl.semaphore_wait(known.at[1], 2)
+    for y in (gy, core):
+        tell(known.at[2], partner, y)
+        tell(known.at[2], partner, lax.rem(y + half, n_gy))
+
+    @pl.when(first_x)
+    def _():
+        tell(known.at[4], 0, core)
+        for y in (gy, core):
+            tell(known.at[4], 0, lax.rem(y + half, n_gy))
+        pl.semaphore_wait(known.at[4], 3)
+        strips_to_first(STRIPS, 0, 0)
 
     strip_left.wait_recv()
     strip_right.wait_recv()
@@ -283,9 +322,9 @@
         final, next_edges[...].reshape(ROWS, 8, 128), ahead(full[ROWS * FACE_Y : ROWS * (FACE_Y + 1)], 1)
     )
 
-    to_up = send(ext.at[:, pl.ds(4, 2)], ext.at[:, pl.ds(0, 2)], 3, gx + 1, gy)
-    to_down = send(ext.at[:, pl.ds(2, 2)], ext.at[:, pl.ds(6, 2)], 4, gx - 1, gy)
-    to_down_face = send(ext.at[FACE_X, 4], last_face, 5, gx - 1, gy)
+    to_up = send(ext.at[:, pl.ds(4, 2)], ext.at[:, pl.ds(0, 2)], 3, 3, gx + 1, gy)
+    to_down = send(ext.at[:, pl.ds(2, 2)], ext.at[:, pl.ds(6, 2)], 4, 4, gx - 1, gy)
+    to_down_face = send(ext.at[FACE_X, 4], last_face, 5, 5, gx - 1, gy)
 
     @pl.when(jnp.logical_not(last_x))
     def _():
@@ -296,51 +335,66 @@
         to_down.start()
         to_down_face.start()
 
-    @pl.when(edge_x)
+    load_shear.wait()
+
+    mine = jnp.where(lax.rem(gy, 2) == 0, lax.div(gy, 2), half + lax.div(gy, 2))
+
+    @pl.when(first_x)
     def _():
         total_cells = cells * n_gy
         offset = shear_ref[0]
-        amount = jnp.where(first_x, lax.rem(total_cells - offset, total_cells), offset)
-        amount_next = lax.rem(amount + total_cells - 1, total_cells)
-        landing = jnp.where(first_x, 6, 0)
-
-        def ship(tiles, field, row, sem):
-            def step(y, carry):
-                send(tiles.at[y], ext.at[field, row], sem, facing, y).start()
-                return carry
-
-            lax.fori_loop(0, n_gy, step, 0)
-
-        def ship_face(tiles):
-            def step(y, carry):
-                send(tiles.at[y], last_face, 5, facing, y).start()
-                return carry
-
-            lax.fori_loop(0, n_gy, step, 0)
-
-        for slot in range(slots):
-            t = slot * n_gy + mine
-            field = lax.div(t, 2)
-
-            @pl.when(t < STRIPS)
-            def _(slot=slot, t=t, field=field):
-                block = strip_in.at[slot, pl.ds(0, 8 * n_gy), :]
-                wait_bytes(block, recv_sems.at[2])
-                strip_in[slot, pl.ds(8 * n_gy, 8 * n_gy), :] = strip_in[slot, pl.ds(0, 8 * n_gy), :]
-                strip_out[slot] = window(strip_in, slot, n_gy, cells, amount, 3)
+        shifts = (lax.rem(total_cells - offset, total_cells), offset)
+
+        def hand(way, tiles, target, arrived):
+            def one(y):
+                @pl.when(jnp.logical_or(way == 0, y != gy))
+                def _():
+                    send(tiles.at[y], target, 8 + way, arrived, last * (1 - way), y).start()
+
+                if way == 1:
+
+                    @pl.when(y == gy)
+                    def _():
+                        pltpu.make_async_copy(tiles.at[y], target, recv_sems.at[arrived]).start()
+
+            everyone(one)
+
+        for way in range(2):
+            for slot in range(slots):
+                t = slot * n_gy + mine
+                field = lax.div(t, 2)
+
+                @pl.when(t < STRIPS - way)
+                def _(way=way, slot=slot, field=field):
+                    wait_bytes(strip_in[way].at[slot, pl.ds(0, 8 * n_gy), :], recv_sems.at[8 + slots * way + slot])
+                    strip_in[way][slot, pl.ds(8 * n_gy, 8 * n_gy), :] = strip_in[way][slot, pl.ds(0, 8 * n_gy), :]
+                    strip_out[way, slot] = window(strip_in[way], slot, n_gy, cells, shifts[way], 3)
+
+                    @pl.when(field == FACE_Y)
+                    def _():
+                        shift = lax.rem(shifts[way] + total_cells - 1, total_cells)
+                        moved[way, slot] = window(strip_in[way], slot, n_gy, cells, shift, 3)
+
+            if way == 0:
+                pl.semaphore_wait(known.at[3], n_gy)
+            for slot in range(slots):
+                t = slot * n_gy + mine
+                field = lax.div(t, 2)
+                landing = 6 * (1 - way) + lax.rem(t, 2)
 
                 @pl.when(t < STRIPS - 1)
-                def _():
-                    ship(strip_out.at[slot], field, landing + lax.rem(t, 2), jnp.where(first_x, 4, 3))
-
-                @pl.when(jnp.logical_and(t == STRIPS - 1, first_x))
-                def _():
-                    ship_face(strip_out.at[slot])
+                def _(way=way, slot=slot, field=field, landing=landing):
+                    hand(way, strip_out.at[way, slot], ext.at[field, landing], 4 - way)
 
                 @pl.when(field == FACE_Y)
-                def _():
-                    moved[slot] = window(strip_in, slot, n_gy, cells, amount_next, 3)
-                    ship(moved.at[slot], NEXT_Y, landing + lax.rem(t, 2), jnp.where(first_x, 4, 3))
+                def _(way=way, slot=slot, landing=landing):
+                    hand(way, moved.at[way, slot], ext.at[NEXT_Y, landing], 4 - way)
+
+                if way == 0:
+
+                    @pl.when(t == STRIPS - 1)
+                    def _(way=way, slot=slot):
+                        hand(way, strip_out.at[way, slot], last_face, 5)
 
     wait_bytes(ext.at[:, pl.ds(0, 2)], recv_sems.at[3])
     wait_bytes(ext.at[:, pl.ds(6, 2)], recv_sems.at[4])
@@ -353,27 +407,17 @@
     for field in range(8):
         lines[ROWS * field : ROWS * field + ROWS] = 0.5 * (ext[field, 2:6] + twice[field][:ROWS])
 
-    def spread(source, target, sem):
-        def step(t, carry):
-            owner = lax.div(t, per)
-
-            @pl.when(owner != gy)
-            def _():
-                send(source(t, owner), target(t), sem, gx, owner).start()
-
-            @pl.when(owner == gy)
-            def _():
-                pltpu.make_async_copy(source(t, owner), target(t), recv_sems.at[sem]).start()
-
-            return carry
-
-        lax.fori_loop(0, LINES, step, 0)
-
-    spread(
-        lambda t, owner: lines.at[t],
-        lambda t: line_in.at[lax.rem(t, per), pl.ds(pl.multiple_of(8 * gy, 8), 8), :],
-        6,
-    )
+    def spread(k, carry):
+        t = lax.rem(k + (gy + half) * per, LINES)
+        slot = lax.rem(t, per)
+        target = line_in.at[slot, pl.ds(pl.multiple_of(8 * gy, 8), 8), :]
+        send(lines.at[t], target, 6, 6, partner, lax.div(t, per)).start()
+        return carry
+
+    pl.semaphore_wait(known.at[2], 4)
+    lax.fori_loop(0, LINES, spread, 0)
+    amounts.wait_recv()
+    levels.wait_recv()
     wait_bytes(line_in.at[:, pl.ds(0, 8 * n_gy), :], recv_sems.at[6])
 
     for slot in range(per):
@@ -384,19 +428,10 @@
         line_out[slot] = (1.0 - weight) * ahead(tiles, 2) + weight * ahead(tiles, 1)
 
     def back(k, carry):
-        y = lax.div(k, per)
+        y = lax.rem(lax.div(k, per) + gy + half, n_gy)
         slot = lax.rem(k, per)
-        source = line_out.at[slot, y]
         target = raw.at[pl.ds(pl.multiple_of(8 * (gy * per + slot), 8), 8), :]
-
-        @pl.when(y != gy)
-        def _():
-            send(source, target, 7, gx, y).start()
-
-        @pl.when(y == gy)
-        def _():
-            pltpu.make_async_copy(source, target, recv_sems.at[7]).start()
-
+        send(line_out.at[slot, y], target, 7, 7, partner, y).start()
         return carry
 
     lax.fori_loop(0, LINES, back, 0)
@@ -408,8 +443,8 @@
                 width = min(128, cells - 128 * chunk)
                 out_ref[field, plane, :, pl.ds(128 * chunk, width)] = part[:, :width]
 
-    strip_left.wait_send()
-    strip_right.wait_send()
+    for copy in (strip_left, strip_right, amounts, levels):
+        copy.wait_send()
 
     @pl.when(jnp.logical_not(last_x))
     def _():
@@ -420,33 +455,29 @@
         to_down.wait_send()
         to_down_face.wait_send()
 
-    @pl.when(edge_x)
-    def _():
-        for count in range(STRIPS - slots, STRIPS + 1):
-            own = sum((slot * n_gy + mine < STRIPS).astype(jnp.int32) for slot in range(slots))
-
-            @pl.when(STRIPS - own == count)
-            def _(count=count):
-                wait_bytes(held.at[pl.ds(0, count)], send_sems.at[2])
-
-        for slot in range(slots):
-            t = slot * n_gy + mine
-            field = lax.div(t, 2)
-
-            @pl.when(t < STRIPS - 1)
-            def _(slot=slot):
-                wait_bytes(strip_out.at[slot], send_sems.at[jnp.where(first_x, 4, 3)])
-
-            @pl.when(jnp.logical_and(t == STRIPS - 1, first_x))
-            def _(slot=slot):
-                wait_bytes(strip_out.at[slot], send_sems.at[5])
-
-            @pl.when(jnp.logical_and(t < STRIPS, field == FACE_Y))
-            def _(slot=slot):
-                wait_bytes(moved.at[slot], send_sems.at[jnp.where(first_x, 4, 3)])
-
-    wait_bytes(lines.at[pl.ds(0, LINES - per)], send_sems.at[6])
-    wait_bytes(lines.at[pl.ds(0, LINES - per)], send_sems.at[7])
+    own = sum((slot * n_gy + mine < STRIPS).astype(jnp.int32) for slot in range(slots))
+    for count in sorted({STRIPS - 1, STRIPS - slots, STRIPS - slots + 1}):
+
+        @pl.when(jnp.logical_or(last_x & (count == STRIPS - 1), first_x & (STRIPS - own == count)))
+        def _(count=count):
+            wait_bytes(held.at[pl.ds(0, count)], send_sems.at[2])
+
+    @pl.when(first_x)
+    def _():
+        for way in range(2):
+            for slot in range(slots):
+                t = slot * n_gy + mine
+
+                @pl.when(t < STRIPS - way)
+                def _(way=way, slot=slot):
+                    wait_bytes(strip_out.at[way, slot, pl.ds(0, n_gy - way)], send_sems.at[8 + way])
+
+                @pl.when(lax.div(t, 2) == FACE_Y)
+                def _(way=way, slot=slot):
+                    wait_bytes(moved.at[way, slot, pl.ds(0, n_gy - way)], send_sems.at[8 + way])
+
+    wait_bytes(lines, send_sems.at[6])
+    wait_bytes(lines, send_sems.at[7])
 
 
 def solution(mesh):
@@ -458,14 +489,18 @@
         per = LINES // n_gy
         slots = -(-STRIPS // n_gy)
         vmem = lambda *shape: pltpu.VMEM(shape, jnp.float32)
-        small = pl.BlockSpec(memory_space=pltpu.SMEM)
         large = pl.BlockSpec(memory_space=pltpu.VMEM)
+        whole = pl.BlockSpec(memory_space=pl.ANY)
         return pl.pallas_call(
             functools.partial(kernel, n_gx, n_gy, cells),
             out_shape=jax.ShapeDtypeStruct(state.shape, jnp.float32),
-            in_specs=[small, small, small, large],
+            in_specs=[whole] * 4,
             out_specs=large,
             scratch_shapes=[
+                pltpu.SMEM((1,), jnp.int32),
+                pltpu.SMEM((ROWS,), jnp.int32),
+                pltpu.SMEM((ROWS,), jnp.int32),
+                vmem(*state.shape),
                 vmem(8 * LINES, 128),
                 vmem(LINES, 8, 128),
                 vmem(9, 8, 8, 128),
@@ -477,13 +512,16 @@
                 vmem(8 * LINES, 128),
                 vmem(8 * ROWS, 128),
                 vmem(slots, 16 * n_gy, 128),
-                vmem(slots, n_gy, 8, 128),
-                vmem(slots, n_gy, 8, 128),
+                vmem(slots, 16 * n_gy, 128),
+                vmem(2, slots, n_gy, 8, 128),
+                vmem(2, slots, n_gy, 8, 128),
                 vmem(per, 16 * n_gy, 128),
                 vmem(per, n_gy, 8, 128),
                 vmem(LINES, 8, 128),
-                pltpu.SemaphoreType.DMA((8,)),
-                pltpu.SemaphoreType.DMA((8,)),
+                pltpu.SemaphoreType.DMA((12,)),
+                pltpu.SemaphoreType.DMA((10 + 2 * slots,)),
+                pltpu.SemaphoreType.DMA((2,)),
+                pltpu.SemaphoreType.REGULAR((5,)),
             ],
             compiler_params=pltpu.CompilerParams(collective_id=0, has_side_effects=True),
         )(shear_offset, remap_shift, frac_index, state)

time: 50.2 us -> 49.2 us (0.980)
  Pallas kernels: 47.8 us -> 46.9 us
    pallas_call x1, Pallas kernels: 47.8 us -> 46.9 us  [shards(): pl.pallas_call(functools.partial(kernel, n_gx, n_gy, cells), out_shape=ja...]
where the time goes in v2:
time: 49.2 us; the launch traced here: 49.1 us
  Pallas kernels  46.9 us (95%)
  local copies, waits for them, and re-layouts  1.57 us (3%)
  between operations  0.66 us (1%)
    pallas_call x1, Pallas kernels, shards(): pl.pallas_call(functools.partial(kernel, n_gx, n_gy, cells), out_shape=ja...  46.9 us
    unnamed x1, local copies, waits for them, and re-layouts  1.57 us

profile of v2, /device:TPU:1, one launch (start us, length us, event | category | flops | bytes accessed | tf_op | source)
XLA Modules:
  0.0 49.1 jit_solution(15854804662802044406)
XLA Ops:
  0.7 46.9 %shard_map.46 = f32[8,2,4,508]{3,2,1,0:T(4,128)} custom-call(s32[1]{0:T(128)S(6)} %copy.6.shear_hbm, s32[4]{0:T(128)} %remap_hbm.1, s32[4]{0:T(128)} %frac_hbm.1, f32[8,2,4,508]{3,2,1,0:T(4,128)} %state_hbm.1), custom_call_target="tpu_custom_call" | custom-call | tf_op jit(solution)/shard_map/pallas_call | solution.py:494
  47.5 1.6 %copy.7 = f32[8,2,4,508]{3,2,1,0:T(4,128)} copy(f32[8,2,4,508]{3,2,1,0:T(4,128)} %shard_map.46) | data formatting | bytes 260096

commit v3 on v2

--- a/solution.py
+++ b/solution.py
@@ -17,7 +17,8 @@
 FACE_X, FACE_Y, FACE_Z, NEXT_Y = 5, 6, 7, 8
 ROWS = 4
 LINES = 8 * ROWS
-STRIPS = 17
+STRIPS = 16
+PAGES = 6
 MESH = pl.DeviceIdType.MESH
 
 
@@ -145,6 +146,7 @@
     shear_ref,
     remap_ref,
     frac_ref,
+    frac_own,
     state_ref,
     raw,
     held,
@@ -156,10 +158,20 @@
     from_right,
     edges,
     next_edges,
-    strip_in_0,
-    strip_in_1,
-    strip_out,
-    moved,
+    line_ghost,
+    line_own,
+    line_far,
+    line_face,
+    near_face,
+    pages,
+    framed,
+    framed_next,
+    ghost_next,
+    framed_face,
+    fresh,
+    fresh_edges,
+    to_next,
+    from_previous,
     line_in,
     line_out,
     lines,
@@ -171,7 +183,6 @@
     gx = lax.axis_index("gx")
     gy = lax.axis_index("gy")
     half = n_gy // 2
-    slots = -(-STRIPS // n_gy)
     per = LINES // n_gy
     left_y = lax.rem(gy + n_gy - 1, n_gy)
     right_y = lax.rem(gy + 1, n_gy)
@@ -179,16 +190,23 @@
     side = gy - inside
     core = gy + 1 - 2 * lax.rem(gy, 2)
     up, down, up_2, down_2 = (side + lax.rem(inside + half + step, half) for step in (2, -2, 4, -4))
+    core_up, core_down = (y + core - gy for y in (up, down))
     partner = lax.rem(gx + n_gx // 2, n_gx)
+    middle = n_gx // 2
     last = n_gx - 1
     first_x = gx == 0
     last_x = gx == last
-    strip_in = (strip_in_0, strip_in_1)
     barrier = pltpu.get_barrier_semaphore()
     load = pltpu.make_async_copy(state_hbm, state_ref, load_sems.at[0])
     load.start()
-    load_shear = pltpu.make_async_copy(shear_hbm, shear_ref, load_sems.at[1])
-    load_shear.start()
+    small_loads = [
+        pltpu.make_async_copy(source, target, load_sems.at[1 + k])
+        for k, (source, target) in enumerate(
+            ((shear_hbm, shear_ref), (frac_hbm, frac_own))
+        )
+    ]
+    for copy in small_loads:
+        copy.start()
 
     def tell(sem, x, y):
         pl.semaphore_signal(sem, inc=1, device_id=(x, y), device_id_type=MESH)
@@ -229,6 +247,9 @@
     @pl.when(first_x)
     def _():
         tell(barrier, 0, lax.rem(gy + half, n_gy))
+
+    @pl.when(jnp.logical_or(first_x, gx == middle))
+    def _():
         everyone(lambda y: tell(barrier, last, y))
 
     load.wait()
@@ -245,44 +266,36 @@
     to_left[...] = raw[pl.ds(0, 64, stride=4), :]
     to_right[...] = raw[pl.ds(3, 64, stride=4), :]
     held[...] = behind(raw[...].reshape(LINES, 8, 128), 2)
-    pl.semaphore_wait(barrier, jnp.where(last_x, 7 + n_gy, 8))
+    pl.semaphore_wait(barrier, jnp.where(last_x, 7 + 2 * n_gy, 8))
     for y in (core, up, down):
         tell(known.at[0], gx, y)
 
-    def strips_to_first(count, base, way):
+    def line_place(buffer, t):
+        return buffer.at[lax.rem(t, per), pl.ds(pl.multiple_of(8 * gy, 8), 8), :]
+
+    @pl.when(last_x)
+    def _():
         def step(k, carry):
-            t = lax.rem(k + lax.div(gy, 2), count)
-            rank = lax.rem(t, n_gy)
-            slot = lax.div(t, n_gy)
-            owner = jnp.where(rank < half, 2 * rank, 2 * (rank - half) + 1)
-            tile = lax.div(t, 2) * ROWS + base + lax.rem(t, 2)
-            tile = jnp.where(t == STRIPS - 1, FACE_X * ROWS + 2, tile)
-            target = strip_in[way].at[slot, pl.ds(pl.multiple_of(8 * gy, 8), 8), :]
-            arrived = 8 + slots * way + slot
-
-            @pl.when(jnp.logical_or(last_x, owner != gy))
-            def _():
-                send(held.at[tile], target, 2, arrived, 0, owner).start()
-
-            @pl.when(jnp.logical_and(first_x, owner == gy))
-            def _():
-                pltpu.make_async_copy(held.at[tile], target, recv_sems.at[arrived]).start()
-
+            u = lax.rem(k + lax.div(gy, 2), STRIPS)
+            t = lax.div(u, 2) * ROWS + 2 + lax.rem(u, 2)
+            send(held.at[t], line_place(line_far, t), 2, 16 + lax.rem(t, per), middle, lax.div(t, per)).start()
             return carry
 
-        lax.fori_loop(0, count, step, 0)
-
-    @pl.when(last_x)
-    def _():
-        strips_to_first(STRIPS - 1, 2, 1)
+        lax.fori_loop(0, STRIPS, step, 0)
         everyone(lambda y: tell(known.at[3], 0, y))
 
+    near_copy = send(held.at[FACE_X * ROWS], near_face, 12, 8, 0, gy)
     strip_left = send(to_left, from_right, 0, 0, gx, left_y)
     strip_right = send(to_right, from_left, 1, 1, gx, right_y)
     strip_left.start()
     strip_right.start()
-    amounts = send(remap_hbm, remap_ref, 10, 8 + 2 * slots, partner, gy)
-    levels = send(frac_hbm, frac_ref, 11, 9 + 2 * slots, partner, gy)
+
+    @pl.when(gx == 1)
+    def _():
+        near_copy.start()
+
+    amounts = send(remap_hbm, remap_ref, 10, 9, partner, gy)
+    levels = send(frac_hbm, frac_ref, 11, 10, partner, gy)
     amounts.start()
     levels.start()
     pl.semaphore_wait(known.at[0], 3)
@@ -296,11 +309,40 @@
 
     @pl.when(first_x)
     def _():
-        tell(known.at[4], 0, core)
         for y in (gy, core):
             tell(known.at[4], 0, lax.rem(y + half, n_gy))
-        pl.semaphore_wait(known.at[4], 3)
-        strips_to_first(STRIPS, 0, 0)
+        for y in (core, up, down, core_up, core_down):
+            tell(known.at[4], 0, y)
+        pl.semaphore_wait(known.at[4], 7)
+
+        def ghosts(k, carry):
+            u = lax.rem(k + lax.div(gy, 2), STRIPS + 1)
+            rank = lax.rem(u, n_gy)
+            slot = lax.div(u, n_gy)
+            owner = jnp.where(rank < half, 2 * rank, 2 * (rank - half) + 1)
+            tile = jnp.where(u == STRIPS, FACE_X * ROWS + 2, lax.div(u, 2) * ROWS + lax.rem(u, 2))
+            target = line_ghost.at[slot, pl.ds(pl.multiple_of(8 * gy, 8), 8), :]
+            arrived = 16 + per + slot
+
+            @pl.when(owner != gy)
+            def _():
+                send(held.at[tile], target, 14, arrived, 0, owner).start()
+
+            @pl.when(owner == gy)
+            def _():
+                pltpu.make_async_copy(held.at[tile], target, recv_sems.at[arrived]).start()
+
+            return carry
+
+        def whole(k, carry):
+            t = lax.rem(k + (gy + half) * per, LINES)
+            send(held.at[t], line_place(line_own, t), 2, 2, middle, lax.div(t, per)).start()
+            return carry
+
+        lax.fori_loop(0, STRIPS + 1, ghosts, 0)
+        lax.fori_loop(0, LINES, whole, 0)
+        near_copy.wait_recv()
+        send(near_face, line_place(line_face, 0), 13, 16 + 2 * per, middle, n_gy - 1).start()
 
     strip_left.wait_recv()
     strip_right.wait_recv()
@@ -335,70 +377,81 @@
         to_down.start()
         to_down_face.start()
 
-    load_shear.wait()
+    for copy in small_loads:
+        copy.wait()
+
+    total_cells = cells * n_gy
+    spare = n_gy - 1
+
+    def fill(page, buffer, slot, amount):
+        pages[page] = window(buffer, slot, n_gy, cells, amount, 3)
+
+    def hand(page, target, sem, arrived, x):
+        everyone(lambda y: send(pages.at[page, y], target, sem, arrived, x, y).start())
+
+    def hand_next(page, target, sem, arrived, x):
+        def one(y):
+            following = lax.rem(y + 1, n_gy)
+            for plane in range(2):
+                source = pages.at[page, following, pl.ds(4 * plane, 1)]
+                send(source, target(plane), sem, arrived, x, y).start()
+
+        everyone(one)
+
+    def next_faces(faces, rows):
+        shape = faces.shape
+        lanes = lax.broadcasted_iota(jnp.int32, shape, 2)
+        places = lax.broadcasted_iota(jnp.int32, shape, 1)
+        follow = pltpu.roll(jnp.broadcast_to(rows[:, 0:1, :], (2 * shape[0], 8, 128)), 123, 2)
+        follow = follow.reshape(shape[0], 2, 8, 128)
+        chosen = jnp.where(places < 4, follow[:, 0], follow[:, 1])
+        return jnp.where((places % 4 == 3) & (lanes == 127), chosen, ahead(faces, 1))
+
+    def wait_left():
+        wait_bytes(ext.at[:, pl.ds(0, 2)], recv_sems.at[3])
+
+    def wait_right():
+        wait_bytes(ext.at[:, pl.ds(6, 2)], recv_sems.at[4])
+        wait_bytes(last_face, recv_sems.at[5])
+
+    places = []
+    for slot in range(per):
+        t = gy * per + slot
+        places.append((slot, lax.div(t, ROWS), lax.rem(t, ROWS)))
+
+    def own_conditions(r, field, row):
+        inner = row < 3 + r
+        return inner, jnp.logical_and(inner, field == FACE_Y), (row == 3) & (field == FACE_X) & (r == 0)
+
+    def far_conditions(r, field, row):
+        inner = row >= 2 + r
+        return inner, jnp.logical_and(inner, field == FACE_Y)
 
     mine = jnp.where(lax.rem(gy, 2) == 0, lax.div(gy, 2), half + lax.div(gy, 2))
-
-    @pl.when(first_x)
-    def _():
-        total_cells = cells * n_gy
-        offset = shear_ref[0]
-        shifts = (lax.rem(total_cells - offset, total_cells), offset)
-
-        def hand(way, tiles, target, arrived):
-            def one(y):
-                @pl.when(jnp.logical_or(way == 0, y != gy))
-                def _():
-                    send(tiles.at[y], target, 8 + way, arrived, last * (1 - way), y).start()
-
-                if way == 1:
-
-                    @pl.when(y == gy)
-                    def _():
-                        pltpu.make_async_copy(tiles.at[y], target, recv_sems.at[arrived]).start()
-
-            everyone(one)
-
-        for way in range(2):
-            for slot in range(slots):
-                t = slot * n_gy + mine
-                field = lax.div(t, 2)
-
-                @pl.when(t < STRIPS - way)
-                def _(way=way, slot=slot, field=field):
-                    wait_bytes(strip_in[way].at[slot, pl.ds(0, 8 * n_gy), :], recv_sems.at[8 + slots * way + slot])
-                    strip_in[way][slot, pl.ds(8 * n_gy, 8 * n_gy), :] = strip_in[way][slot, pl.ds(0, 8 * n_gy), :]
-                    strip_out[way, slot] = window(strip_in[way], slot, n_gy, cells, shifts[way], 3)
-
-                    @pl.when(field == FACE_Y)
-                    def _():
-                        shift = lax.rem(shifts[way] + total_cells - 1, total_cells)
-                        moved[way, slot] = window(strip_in[way], slot, n_gy, cells, shift, 3)
-
-            if way == 0:
-                pl.semaphore_wait(known.at[3], n_gy)
-            for slot in range(slots):
-                t = slot * n_gy + mine
-                field = lax.div(t, 2)
-                landing = 6 * (1 - way) + lax.rem(t, 2)
-
-                @pl.when(t < STRIPS - 1)
-                def _(way=way, slot=slot, field=field, landing=landing):
-                    hand(way, strip_out.at[way, slot], ext.at[field, landing], 4 - way)
-
-                @pl.when(field == FACE_Y)
-                def _(way=way, slot=slot, landing=landing):
-                    hand(way, moved.at[way, slot], ext.at[NEXT_Y, landing], 4 - way)
-
-                if way == 0:
-
-                    @pl.when(t == STRIPS - 1)
-                    def _(way=way, slot=slot):
-                        hand(way, strip_out.at[way, slot], last_face, 5)
-
-    wait_bytes(ext.at[:, pl.ds(0, 2)], recv_sems.at[3])
-    wait_bytes(ext.at[:, pl.ds(6, 2)], recv_sems.at[4])
-    wait_bytes(last_face, recv_sems.at[5])
+    ghost_places = []
+    for slot in range(-(-(STRIPS + 1) // n_gy)):
+        u = slot * n_gy + mine
+        ghost_places.append((slot, u, lax.div(u, 2) == FACE_Y))
+
+    @pl.when(first_x)
+    def _():
+        wait_right()
+        ext[:, 0:2] = ext[:, 2:4]
+
+    @pl.when(jnp.logical_not(first_x))
+    def _():
+        wait_left()
+
+    @pl.when(jnp.logical_not(jnp.logical_or(first_x, last_x)))
+    def _():
+        wait_right()
+
+    @pl.when(last_x)
+    def _():
+        wait_bytes(ext.at[pl.ds(0, 8), pl.ds(6, 2)], recv_sems.at[4])
+        wait_bytes(last_face, recv_sems.at[5])
+        wait_bytes(ghost_next.at[:, pl.ds(0, 1)], recv_sems.at[17 + 2 * per])
+        ext[NEXT_Y, 6:8] = next_faces(ext[FACE_Y, 6:8], ghost_next[...])
 
     fields = [ext[field] for field in range(8)]
     fields[FACE_X] = jnp.concatenate([fields[FACE_X], last_face[...][None]], axis=0)
@@ -411,31 +464,175 @@
         t = lax.rem(k + (gy + half) * per, LINES)
         slot = lax.rem(t, per)
         target = line_in.at[slot, pl.ds(pl.multiple_of(8 * gy, 8), 8), :]
-        send(lines.at[t], target, 6, 6, partner, lax.div(t, per)).start()
+
+        @pl.when(jnp.logical_not(first_x) | (lax.rem(t, ROWS) >= 2))
+        def _():
+            send(lines.at[t], target, 6, 6, partner, lax.div(t, per)).start()
+
         return carry
 
-    pl.semaphore_wait(known.at[2], 4)
+    @pl.when(jnp.logical_not(first_x))
+    def _():
+        pl.semaphore_wait(known.at[2], 4)
+
     lax.fori_loop(0, LINES, spread, 0)
+
+    @pl.when(first_x)
+    def _():
+        pl.semaphore_wait(known.at[2], 4)
+
+    @pl.when(first_x)
+    def _():
+        ghost_amount = lax.rem(total_cells - shear_ref[0], total_cells)
+        for slot, u, faces in ghost_places:
+
+            @pl.when(u <= STRIPS)
+            def _(slot=slot):
+                wait_bytes(line_ghost.at[slot, pl.ds(0, 8 * n_gy), :], recv_sems.at[16 + per + slot])
+                line_ghost[slot, pl.ds(8 * n_gy, 8 * n_gy), :] = line_ghost[slot, pl.ds(0, 8 * n_gy), :]
+                fill(4 * per + slot, line_ghost, slot, ghost_amount)
+
+        pl.semaphore_wait(known.at[3], n_gy)
+        for slot, u, faces in ghost_places:
+
+            @pl.when(u < STRIPS)
+            def _(slot=slot, u=u):
+                hand(4 * per + slot, ext.at[lax.div(u, 2), 6 + lax.rem(u, 2)], 8, 4, last)
+
+            @pl.when(faces)
+            def _(slot=slot, u=u):
+                row = lax.rem(u, 2)
+                hand_next(4 * per + slot, lambda plane: ghost_next.at[2 * row + plane, pl.ds(0, 1)], 15, 17 + 2 * per, last)
+
+            @pl.when(u == STRIPS)
+            def _(slot=slot):
+                hand(4 * per + slot, last_face, 8, 5, last)
+
     amounts.wait_recv()
     levels.wait_recv()
-    wait_bytes(line_in.at[:, pl.ds(0, 8 * n_gy), :], recv_sems.at[6])
-
+
+    @pl.when(gx == middle)
+    def _():
+        wait_bytes(line_own.at[:, pl.ds(0, 8 * n_gy), :], recv_sems.at[2])
+        line_own[:, pl.ds(8 * n_gy, 8 * n_gy), :] = line_own[:, pl.ds(0, 8 * n_gy), :]
+        for slot, field, row in places:
+
+            def frame(r, carry, slot=slot, field=field, row=row):
+                inner, faces, edge = own_conditions(r, field, row)
+                page = r * per + slot
+
+                @pl.when(jnp.logical_or(inner, edge))
+                def _():
+                    fill(page, line_own, slot, remap_ref[r])
+
+                @pl.when(inner)
+                def _():
+                    hand(page, framed.at[r, field, row + 2 - r], 9, 11 + r, 0)
+
+                @pl.when(edge)
+                def _():
+                    hand(page, framed_face.at[0], 9, 13, 0)
+
+                @pl.when(faces)
+                def _():
+                    start = 2 * (row + 2 - r)
+                    hand_next(page, lambda plane: framed_next.at[r, start + plane, pl.ds(0, 1)], 15, 18 + 2 * per + r, 0)
+
+                return carry
+
+            lax.fori_loop(0, 2, frame, 0)
+
+        @pl.when(gy == spare)
+        def _():
+            wait_bytes(line_face.at[0, pl.ds(0, 8 * n_gy), :], recv_sems.at[16 + 2 * per])
+            line_face[0, pl.ds(8 * n_gy, 8 * n_gy), :] = line_face[0, pl.ds(0, 8 * n_gy), :]
+            fill(5 * per, line_face, 0, remap_ref[1])
+            hand(5 * per, framed_face.at[1], 9, 14, 0)
+
+        for slot, field, row in places:
+
+            @pl.when(row >= 2)
+            def _(slot=slot, field=field, row=row):
+                wait_bytes(line_far.at[slot, pl.ds(0, 8 * n_gy), :], recv_sems.at[16 + slot])
+                line_far[slot, pl.ds(8 * n_gy, 8 * n_gy), :] = line_far[slot, pl.ds(0, 8 * n_gy), :]
+
+                def frame(r, carry):
+                    inner, faces = far_conditions(r, field, row)
+                    page = (2 + r) * per + slot
+                    amount = lax.rem(remap_ref[r] + shear_ref[0], total_cells)
+
+                    @pl.when(inner)
+                    def _():
+                        fill(page, line_far, slot, amount)
+                        hand(page, framed.at[r, field, row - 2 - r], 9, 11 + r, 0)
+
+                    @pl.when(faces)
+                    def _():
+                        start = 2 * (row - 2 - r)
+                        hand_next(page, lambda plane: framed_next.at[r, start + plane, pl.ds(0, 1)], 15, 18 + 2 * per + r, 0)
+
+                    return carry
+
+                lax.fori_loop(0, 2, frame, 0)
+
+
+    expected = [jnp.logical_or(gx != middle, row >= 2) for _, _, row in places]
     for slot in range(per):
-        row = lax.rem(gy * per + slot, ROWS)
-        line_in[slot, pl.ds(8 * n_gy, 8 * n_gy), :] = line_in[slot, pl.ds(0, 8 * n_gy), :]
-        tiles = window(line_in, slot, n_gy, cells, remap_ref[row], 2)
-        weight = (frac_ref[row].astype(jnp.float32) + 0.5) / FRAC
-        line_out[slot] = (1.0 - weight) * ahead(tiles, 2) + weight * ahead(tiles, 1)
-
-    def back(k, carry):
-        y = lax.rem(lax.div(k, per) + gy + half, n_gy)
-        slot = lax.rem(k, per)
-        target = raw.at[pl.ds(pl.multiple_of(8 * (gy * per + slot), 8), 8), :]
-        send(line_out.at[slot, y], target, 7, 7, partner, y).start()
-        return carry
-
-    lax.fori_loop(0, LINES, back, 0)
-    wait_bytes(raw, recv_sems.at[7])
+
+        @pl.when(expected[slot])
+        def _(slot=slot):
+            wait_bytes(line_in.at[slot, pl.ds(0, 8 * n_gy), :], recv_sems.at[6])
+
+    for slot in range(per):
+
+        @pl.when(expected[slot])
+        def _(slot=slot):
+            row = lax.rem(gy * per + slot, ROWS)
+            line_in[slot, pl.ds(8 * n_gy, 8 * n_gy), :] = line_in[slot, pl.ds(0, 8 * n_gy), :]
+            tiles = window(line_in, slot, n_gy, cells, remap_ref[row], 2)
+            weight = (frac_ref[row].astype(jnp.float32) + 0.5) / FRAC
+            line_out[slot] = (1.0 - weight) * ahead(tiles, 2) + weight * ahead(tiles, 1)
+            target = raw.at[pl.ds(pl.multiple_of(8 * (gy * per + slot), 8), 8), :]
+            everyone(lambda y: send(line_out.at[slot, y], target, 7, 7, partner, y).start())
+
+    next_copy = send(to_next, from_previous, 12, 15, 0, right_y)
+
+    @pl.when(first_x)
+    def _():
+        for r in range(2):
+            wait_bytes(framed.at[r], recv_sems.at[11 + r])
+            wait_bytes(framed_face.at[r], recv_sems.at[13 + r])
+            fields = [framed[r, field] for field in range(8)]
+            fields[FACE_X] = jnp.concatenate([fields[FACE_X], framed_face[r][None]], axis=0)
+            wait_bytes(framed_next.at[r, :, pl.ds(0, 1)], recv_sems.at[18 + 2 * per + r])
+            once = euler(fields, next_faces(fields[FACE_Y], framed_next[r]))
+            twice = euler(once, ahead(once[FACE_Y], 1))
+            for field in range(8):
+                fresh[pl.ds(64 * r + 8 * field, 8), :] = 0.5 * (framed[r, field, 2] + twice[field][0])
+        to_next[...] = fresh[pl.ds(3, 32, stride=4), :]
+        next_copy.start()
+        next_copy.wait_recv()
+        reach = cells % 128 + 1
+        fresh_edges[pl.ds(0, 32, stride=4), :] = pltpu.roll(from_previous[...], 129 - reach, 1)
+
+    @pl.when(jnp.logical_not(first_x))
+    def _():
+        wait_bytes(raw, recv_sems.at[7])
+
+    @pl.when(first_x)
+    def _():
+        wait_bytes(raw.at[pl.ds(0, 4 * LINES)], recv_sems.at[7])
+        tiles = fresh[...].reshape(16, 8, 128)
+        lanes = lax.broadcasted_iota(jnp.int32, tiles.shape, 2)
+        chunks = lax.broadcasted_iota(jnp.int32, tiles.shape, 1) % 4
+        tiles = jnp.where((chunks == 0) & (lanes == 1), fresh_edges[...].reshape(16, 8, 128), tiles)
+        here, there = ahead(tiles, 2), ahead(tiles, 1)
+        for r in range(2):
+            weight = (frac_own[r].astype(jnp.float32) + 0.5) / FRAC
+            mixed = (1.0 - weight) * here[8 * r : 8 * r + 8] + weight * there[8 * r : 8 * r + 8]
+            for field in range(8):
+                raw[pl.ds(32 * field + 8 * r, 8), :] = mixed[field]
+
     for field in range(8):
         for plane in range(2):
             for chunk in range(4):
@@ -446,6 +643,10 @@
     for copy in (strip_left, strip_right, amounts, levels):
         copy.wait_send()
 
+    @pl.when(gx == 1)
+    def _():
+        near_copy.wait_send()
+
     @pl.when(jnp.logical_not(last_x))
     def _():
         to_up.wait_send()
@@ -455,29 +656,64 @@
         to_down.wait_send()
         to_down_face.wait_send()
 
-    own = sum((slot * n_gy + mine < STRIPS).astype(jnp.int32) for slot in range(slots))
-    for count in sorted({STRIPS - 1, STRIPS - slots, STRIPS - slots + 1}):
-
-        @pl.when(jnp.logical_or(last_x & (count == STRIPS - 1), first_x & (STRIPS - own == count)))
-        def _(count=count):
-            wait_bytes(held.at[pl.ds(0, count)], send_sems.at[2])
-
-    @pl.when(first_x)
-    def _():
-        for way in range(2):
-            for slot in range(slots):
-                t = slot * n_gy + mine
-
-                @pl.when(t < STRIPS - way)
-                def _(way=way, slot=slot):
-                    wait_bytes(strip_out.at[way, slot, pl.ds(0, n_gy - way)], send_sems.at[8 + way])
-
-                @pl.when(lax.div(t, 2) == FACE_Y)
-                def _(way=way, slot=slot):
-                    wait_bytes(moved.at[way, slot, pl.ds(0, n_gy - way)], send_sems.at[8 + way])
-
-    wait_bytes(lines, send_sems.at[6])
-    wait_bytes(lines, send_sems.at[7])
+    @pl.when(last_x)
+    def _():
+        wait_bytes(held.at[pl.ds(0, STRIPS)], send_sems.at[2])
+
+    def left(condition, page, sem):
+        @pl.when(condition)
+        def _():
+            wait_bytes(pages.at[page], send_sems.at[sem])
+
+    def left_next(condition):
+        @pl.when(condition)
+        def _():
+            wait_bytes(pages.at[0, pl.ds(0, n_gy // 4)], send_sems.at[15])
+
+    @pl.when(first_x)
+    def _():
+        wait_bytes(held, send_sems.at[2])
+        wait_bytes(near_face, send_sems.at[13])
+        next_copy.wait_send()
+        count_own = sum((u <= STRIPS).astype(jnp.int32) for _, u, _ in ghost_places)
+        for count in range(len(ghost_places) + 1):
+
+            @pl.when(count_own == count)
+            def _(count=count):
+                wait_bytes(held.at[pl.ds(0, STRIPS + 1 - count)], send_sems.at[14])
+
+        for slot, u, faces in ghost_places:
+            left(u <= STRIPS, 4 * per + slot, 8)
+            left_next(faces)
+
+    @pl.when(gx == middle)
+    def _():
+        @pl.when(gy == spare)
+        def _():
+            wait_bytes(pages.at[5 * per], send_sems.at[9])
+
+        for slot, field, row in places:
+            for r in range(2):
+                inner, faces, edge = own_conditions(r, field, row)
+                left(jnp.logical_or(inner, edge), r * per + slot, 9)
+                left_next(faces)
+                inner, faces = far_conditions(r, field, row)
+                left(inner, (2 + r) * per + slot, 9)
+                left_next(faces)
+
+    @pl.when(first_x)
+    def _():
+        wait_bytes(lines.at[pl.ds(0, LINES // 2)], send_sems.at[6])
+
+    @pl.when(jnp.logical_not(first_x))
+    def _():
+        wait_bytes(lines, send_sems.at[6])
+
+    for slot in range(per):
+
+        @pl.when(expected[slot])
+        def _(slot=slot):
+            wait_bytes(line_out.at[slot], send_sems.at[7])
 
 
 def solution(mesh):
@@ -487,7 +723,6 @@
     def shards(state, shear_offset, remap_shift, frac_index):
         cells = state.shape[3]
         per = LINES // n_gy
-        slots = -(-STRIPS // n_gy)
         vmem = lambda *shape: pltpu.VMEM(shape, jnp.float32)
         large = pl.BlockSpec(memory_space=pltpu.VMEM)
         whole = pl.BlockSpec(memory_space=pl.ANY)
@@ -498,6 +733,7 @@
             out_specs=large,
             scratch_shapes=[
                 pltpu.SMEM((1,), jnp.int32),
+                pltpu.SMEM((ROWS,), jnp.int32),
                 pltpu.SMEM((ROWS,), jnp.int32),
                 pltpu.SMEM((ROWS,), jnp.int32),
                 vmem(*state.shape),
@@ -511,16 +747,26 @@
                 vmem(64, 128),
                 vmem(8 * LINES, 128),
                 vmem(8 * ROWS, 128),
-                vmem(slots, 16 * n_gy, 128),
-                vmem(slots, 16 * n_gy, 128),
-                vmem(2, slots, n_gy, 8, 128),
-                vmem(2, slots, n_gy, 8, 128),
+                vmem(per, 16 * n_gy, 128),
+                vmem(per, 16 * n_gy, 128),
+                vmem(per, 16 * n_gy, 128),
+                vmem(1, 16 * n_gy, 128),
+                vmem(8, 128),
+                vmem(PAGES * per, n_gy, 8, 128),
+                vmem(2, 8, 5, 8, 128),
+                vmem(2, 10, 8, 128),
+                vmem(4, 8, 128),
+                vmem(2, 8, 128),
+                vmem(128, 128),
+                vmem(128, 128),
+                vmem(32, 128),
+                vmem(32, 128),
                 vmem(per, 16 * n_gy, 128),
                 vmem(per, n_gy, 8, 128),
                 vmem(LINES, 8, 128),
-                pltpu.SemaphoreType.DMA((12,)),
-                pltpu.SemaphoreType.DMA((10 + 2 * slots,)),
-                pltpu.SemaphoreType.DMA((2,)),
+                pltpu.SemaphoreType.DMA((16,)),
+                pltpu.SemaphoreType.DMA((20 + 2 * per,)),
+                pltpu.SemaphoreType.DMA((3,)),
                 pltpu.SemaphoreType.REGULAR((5,)),
             ],
             compiler_params=pltpu.CompilerParams(collective_id=0, has_side_effects=True),

time: 49.2 us -> 44.9 us (0.913)
  the two profiles are of different devices: /device:TPU:1 before, /device:TPU:4 now
where the time goes in v3:
time: 44.9 us; the launch traced here: 44.7 us
  Pallas kernels  42.5 us (95%)
  local copies, waits for them, and re-layouts  1.57 us (3%)
  between operations  0.66 us (1%)
    pallas_call x1, Pallas kernels, shards(): pl.pallas_call(functools.partial(kernel, n_gx, n_gy, cells), out_shape=ja...  42.5 us
    unnamed x1, local copies, waits for them, and re-layouts  1.57 us

profile of v3, /device:TPU:4, one launch (start us, length us, event | category | flops | bytes accessed | tf_op | source)
XLA Modules:
  0.0 44.7 jit_solution(9019636891541357210)
XLA Ops:
  0.7 42.5 %shard_map.46 = f32[8,2,4,508]{3,2,1,0:T(4,128)} custom-call(s32[1]{0:T(128)S(6)} %copy.6.shear_hbm, s32[4]{0:T(128)} %remap_hbm.1, s32[4]{0:T(128)} %frac_hbm.1, f32[8,2,4,508]{3,2,1,0:T(4,128)} %state_hbm.1), custom_call_target="tpu_custom_call" | custom-call | tf_op jit(solution)/shard_map/pallas_call | solution.py:729
  43.1 1.6 %copy.7 = f32[8,2,4,508]{3,2,1,0:T(4,128)} copy(f32[8,2,4,508]{3,2,1,0:T(4,128)} %shard_map.46) | data formatting | bytes 260096

commit v4 on v3

--- a/solution.py
+++ b/solution.py
@@ -146,6 +146,7 @@
     shear_ref,
     remap_ref,
     frac_ref,
+    remap_own,
     frac_own,
     state_ref,
     raw,
@@ -190,7 +191,6 @@
     side = gy - inside
     core = gy + 1 - 2 * lax.rem(gy, 2)
     up, down, up_2, down_2 = (side + lax.rem(inside + half + step, half) for step in (2, -2, 4, -4))
-    core_up, core_down = (y + core - gy for y in (up, down))
     partner = lax.rem(gx + n_gx // 2, n_gx)
     middle = n_gx // 2
     last = n_gx - 1
@@ -202,7 +202,7 @@
     small_loads = [
         pltpu.make_async_copy(source, target, load_sems.at[1 + k])
         for k, (source, target) in enumerate(
-            ((shear_hbm, shear_ref), (frac_hbm, frac_own))
+            ((shear_hbm, shear_ref), (remap_hbm, remap_own), (frac_hbm, frac_own))
         )
     ]
     for copy in small_loads:
@@ -231,10 +231,27 @@
     def wait_bytes(ref, sem):
         pltpu.make_async_copy(ref, ref, sem).wait()
 
-    for y in (left_y, right_y, up, down):
-        tell(barrier, gx, y)
-    for y in (gy, lax.rem(gy + half, n_gy)):
-        tell(barrier, partner, y)
+    @pl.when(first_x)
+    def _():
+        def step(k, carry):
+            tell(barrier, 0, lax.rem(gy + k, n_gy))
+            return carry
+
+        lax.fori_loop(1, n_gy, step, 0)
+
+    @pl.when(gx == middle)
+    def _():
+        everyone(lambda y: tell(barrier, 0, y))
+
+    @pl.when(jnp.logical_not(first_x))
+    def _():
+        for y in (left_y, right_y, up, down):
+            tell(barrier, gx, y)
+
+    @pl.when(gx != middle)
+    def _():
+        for y in (gy, lax.rem(gy + half, n_gy)):
+            tell(barrier, partner, y)
 
     @pl.when(jnp.logical_not(first_x))
     def _():
@@ -245,10 +262,6 @@
         tell(barrier, gx + 1, gy)
 
     @pl.when(first_x)
-    def _():
-        tell(barrier, 0, lax.rem(gy + half, n_gy))
-
-    @pl.when(jnp.logical_or(first_x, gx == middle))
     def _():
         everyone(lambda y: tell(barrier, last, y))
 
@@ -266,9 +279,13 @@
     to_left[...] = raw[pl.ds(0, 64, stride=4), :]
     to_right[...] = raw[pl.ds(3, 64, stride=4), :]
     held[...] = behind(raw[...].reshape(LINES, 8, 128), 2)
-    pl.semaphore_wait(barrier, jnp.where(last_x, 7 + 2 * n_gy, 8))
-    for y in (core, up, down):
-        tell(known.at[0], gx, y)
+    pl.semaphore_wait(barrier, jnp.where(last_x, 7 + n_gy, jnp.where(first_x, 2 * n_gy, 8)))
+
+    @pl.when(jnp.logical_not(first_x))
+    def _():
+        for y in (core, up, down):
+            tell(known.at[0], gx, y)
+
 
     def line_place(buffer, t):
         return buffer.at[lax.rem(t, per), pl.ds(pl.multiple_of(8 * gy, 8), 8), :]
@@ -278,7 +295,7 @@
         def step(k, carry):
             u = lax.rem(k + lax.div(gy, 2), STRIPS)
             t = lax.div(u, 2) * ROWS + 2 + lax.rem(u, 2)
-            send(held.at[t], line_place(line_far, t), 2, 16 + lax.rem(t, per), middle, lax.div(t, per)).start()
+            send(held.at[t], line_place(line_far, t), 2, 16 + lax.rem(t, per), 0, lax.div(t, per)).start()
             return carry
 
         lax.fori_loop(0, STRIPS, step, 0)
@@ -298,23 +315,20 @@
     levels = send(frac_hbm, frac_ref, 11, 10, partner, gy)
     amounts.start()
     levels.start()
-    pl.semaphore_wait(known.at[0], 3)
-    if half > 4:
-        for y in (up_2, down_2):
-            tell(known.at[1], gx, y)
-        pl.semaphore_wait(known.at[1], 2)
+    @pl.when(jnp.logical_not(first_x))
+    def _():
+        pl.semaphore_wait(known.at[0], 3)
+        if half > 4:
+            for y in (up_2, down_2):
+                tell(known.at[1], gx, y)
+            pl.semaphore_wait(known.at[1], 2)
+
     for y in (gy, core):
         tell(known.at[2], partner, y)
         tell(known.at[2], partner, lax.rem(y + half, n_gy))
 
     @pl.when(first_x)
     def _():
-        for y in (gy, core):
-            tell(known.at[4], 0, lax.rem(y + half, n_gy))
-        for y in (core, up, down, core_up, core_down):
-            tell(known.at[4], 0, y)
-        pl.semaphore_wait(known.at[4], 7)
-
         def ghosts(k, carry):
             u = lax.rem(k + lax.div(gy, 2), STRIPS + 1)
             rank = lax.rem(u, n_gy)
@@ -339,8 +353,8 @@
             send(held.at[t], line_place(line_own, t), 2, 2, middle, lax.div(t, per)).start()
             return carry
 
+        lax.fori_loop(0, LINES, whole, 0)
         lax.fori_loop(0, STRIPS + 1, ghosts, 0)
-        lax.fori_loop(0, LINES, whole, 0)
         near_copy.wait_recv()
         send(near_face, line_place(line_face, 0), 13, 16 + 2 * per, middle, n_gy - 1).start()
 
@@ -386,15 +400,29 @@
     def fill(page, buffer, slot, amount):
         pages[page] = window(buffer, slot, n_gy, cells, amount, 3)
 
+    def deliver(source, target, sem, arrived, x, y):
+        if x == "self":
+
+            @pl.when(y != gy)
+            def _():
+                send(source, target, sem, arrived, 0, y).start()
+
+            @pl.when(y == gy)
+            def _():
+                pltpu.make_async_copy(source, target, recv_sems.at[arrived]).start()
+
+        else:
+            send(source, target, sem, arrived, x, y).start()
+
     def hand(page, target, sem, arrived, x):
-        everyone(lambda y: send(pages.at[page, y], target, sem, arrived, x, y).start())
+        everyone(lambda y: deliver(pages.at[page, y], target, sem, arrived, x, y))
 
     def hand_next(page, target, sem, arrived, x):
         def one(y):
             following = lax.rem(y + 1, n_gy)
             for plane in range(2):
                 source = pages.at[page, following, pl.ds(4 * plane, 1)]
-                send(source, target(plane), sem, arrived, x, y).start()
+                deliver(source, target(plane), sem, arrived, x, y)
 
         everyone(one)
 
@@ -508,6 +536,32 @@
             def _(slot=slot):
                 hand(4 * per + slot, last_face, 8, 5, last)
 
+        for slot, field, row in places:
+
+            @pl.when(row >= 2)
+            def _(slot=slot, field=field, row=row):
+                wait_bytes(line_far.at[slot, pl.ds(0, 8 * n_gy), :], recv_sems.at[16 + slot])
+                line_far[slot, pl.ds(8 * n_gy, 8 * n_gy), :] = line_far[slot, pl.ds(0, 8 * n_gy), :]
+
+                def frame(r, carry):
+                    inner, faces = far_conditions(r, field, row)
+                    page = (2 + r) * per + slot
+                    amount = lax.rem(remap_own[r] + shear_ref[0], total_cells)
+
+                    @pl.when(inner)
+                    def _():
+                        fill(page, line_far, slot, amount)
+                        hand(page, framed.at[r, field, row - 2 - r], 9, 11 + r, "self")
+
+                    @pl.when(faces)
+                    def _():
+                        start = 2 * (row - 2 - r)
+                        hand_next(page, lambda plane: framed_next.at[r, start + plane, pl.ds(0, 1)], 15, 18 + 2 * per + r, "self")
+
+                    return carry
+
+                lax.fori_loop(0, 2, frame, 0)
+
     amounts.wait_recv()
     levels.wait_recv()
 
@@ -548,33 +602,6 @@
             line_face[0, pl.ds(8 * n_gy, 8 * n_gy), :] = line_face[0, pl.ds(0, 8 * n_gy), :]
             fill(5 * per, line_face, 0, remap_ref[1])
             hand(5 * per, framed_face.at[1], 9, 14, 0)
-
-        for slot, field, row in places:
-
-            @pl.when(row >= 2)
-            def _(slot=slot, field=field, row=row):
-                wait_bytes(line_far.at[slot, pl.ds(0, 8 * n_gy), :], recv_sems.at[16 + slot])
-                line_far[slot, pl.ds(8 * n_gy, 8 * n_gy), :] = line_far[slot, pl.ds(0, 8 * n_gy), :]
-
-                def frame(r, carry):
-                    inner, faces = far_conditions(r, field, row)
-                    page = (2 + r) * per + slot
-                    amount = lax.rem(remap_ref[r] + shear_ref[0], total_cells)
-
-                    @pl.when(inner)
-                    def _():
-                        fill(page, line_far, slot, amount)
-                        hand(page, framed.at[r, field, row - 2 - r], 9, 11 + r, 0)
-
-                    @pl.when(faces)
-                    def _():
-                        start = 2 * (row - 2 - r)
-                        hand_next(page, lambda plane: framed_next.at[r, start + plane, pl.ds(0, 1)], 15, 18 + 2 * per + r, 0)
-
-                    return carry
-
-                lax.fori_loop(0, 2, frame, 0)
-
 
     expected = [jnp.logical_or(gx != middle, row >= 2) for _, _, row in places]
     for slot in range(per):
@@ -633,12 +660,7 @@
             for field in range(8):
                 raw[pl.ds(32 * field + 8 * r, 8), :] = mixed[field]
 
-    for field in range(8):
-        for plane in range(2):
-            for chunk in range(4):
-                part = raw[pl.ds(field * 32 + plane * 4 + chunk, ROWS, stride=8), :]
-                width = min(128, cells - 128 * chunk)
-                out_ref[field, plane, :, pl.ds(128 * chunk, width)] = part[:, :width]
+    out_ref[...] = raw[...]
 
     for copy in (strip_left, strip_right, amounts, levels):
         copy.wait_send()
@@ -665,10 +687,10 @@
         def _():
             wait_bytes(pages.at[page], send_sems.at[sem])
 
-    def left_next(condition):
+    def left_next(condition, one_less=0):
         @pl.when(condition)
         def _():
-            wait_bytes(pages.at[0, pl.ds(0, n_gy // 4)], send_sems.at[15])
+            wait_bytes(pages.at[pl.ds(0, 2), pl.ds(0, n_gy - one_less), pl.ds(0, 1)], send_sems.at[15])
 
     @pl.when(first_x)
     def _():
@@ -686,6 +708,16 @@
             left(u <= STRIPS, 4 * per + slot, 8)
             left_next(faces)
 
+        for slot, field, row in places:
+            for r in range(2):
+                inner, faces = far_conditions(r, field, row)
+                left_next(faces, 1)
+
+                @pl.when(inner)
+                def _(slot=slot, r=r):
+                    wait_bytes(pages.at[(2 + r) * per + slot, pl.ds(0, n_gy - 1)], send_sems.at[9])
+
+
     @pl.when(gx == middle)
     def _():
         @pl.when(gy == spare)
@@ -697,9 +729,6 @@
                 inner, faces, edge = own_conditions(r, field, row)
                 left(jnp.logical_or(inner, edge), r * per + slot, 9)
                 left_next(faces)
-                inner, faces = far_conditions(r, field, row)
-                left(inner, (2 + r) * per + slot, 9)
-                left_next(faces)
 
     @pl.when(first_x)
     def _():
@@ -714,6 +743,16 @@
         @pl.when(expected[slot])
         def _(slot=slot):
             wait_bytes(line_out.at[slot], send_sems.at[7])
+
+
+def unpack(tiles_ref, out_ref):
+    cells = out_ref.shape[3]
+    for field in range(8):
+        for plane in range(2):
+            for chunk in range(4):
+                part = tiles_ref[pl.ds(field * 32 + plane * 4 + chunk, ROWS, stride=8), :]
+                width = min(128, cells - 128 * chunk)
+                out_ref[field, plane, :, pl.ds(128 * chunk, width)] = part[:, :width]
 
 
 def solution(mesh):
@@ -725,14 +764,15 @@
         per = LINES // n_gy
         vmem = lambda *shape: pltpu.VMEM(shape, jnp.float32)
         large = pl.BlockSpec(memory_space=pltpu.VMEM)
-        whole = pl.BlockSpec(memory_space=pl.ANY)
-        return pl.pallas_call(
+        whole = pl.BlockSpec(memory_space=pltpu.HBM)
+        tiles = pl.pallas_call(
             functools.partial(kernel, n_gx, n_gy, cells),
-            out_shape=jax.ShapeDtypeStruct(state.shape, jnp.float32),
+            out_shape=pltpu.VMEM((8 * LINES, 128), jnp.float32),
             in_specs=[whole] * 4,
             out_specs=large,
             scratch_shapes=[
                 pltpu.SMEM((1,), jnp.int32),
+                pltpu.SMEM((ROWS,), jnp.int32),
                 pltpu.SMEM((ROWS,), jnp.int32),
                 pltpu.SMEM((ROWS,), jnp.int32),
                 pltpu.SMEM((ROWS,), jnp.int32),
@@ -766,11 +806,20 @@
                 vmem(LINES, 8, 128),
                 pltpu.SemaphoreType.DMA((16,)),
                 pltpu.SemaphoreType.DMA((20 + 2 * per,)),
-                pltpu.SemaphoreType.DMA((3,)),
-                pltpu.SemaphoreType.REGULAR((5,)),
+                pltpu.SemaphoreType.DMA((4,)),
+                pltpu.SemaphoreType.REGULAR((4,)),
             ],
-            compiler_params=pltpu.CompilerParams(collective_id=0, has_side_effects=True),
+            compiler_params=pltpu.CompilerParams(
+                collective_id=0, has_side_effects=True
+            ),
         )(shear_offset, remap_shift, frac_index, state)
+        return pl.pallas_call(
+            unpack,
+            out_shape=jax.ShapeDtypeStruct(state.shape, jnp.float32),
+            in_specs=[large],
+            out_specs=large,
+            compiler_params=pltpu.CompilerParams(vmem_limit_bytes=8 * 2**20),
+        )(tiles)
 
     placed = (P(None, None, "gx", "gy"), P(), P("gx"), P("gx"))
     return jax.shard_map(shards, mesh=mesh, in_specs=placed, out_specs=P(None, None, "gx", "gy"), check_vma=False)

time: 44.9 us -> 40.3 us (0.90)
  Pallas kernels: 42.5 us -> 39.6 us
  local copies, waits for them, and re-layouts: 1.57 us -> 0 us
    pallas_call x1 -> x2, Pallas kernels: 42.5 us -> 39.6 us  [the longest x1 38.9 us: shards(): pl.pallas_call(functools.partial(kernel, n_gx, n_gy, cells), out_shape=pl...]
    unnamed x1 -> x0, local copies, waits for them, and re-layouts: 1.57 us -> none
where the time goes in v4:
time: 40.3 us; the launch traced here: 40.2 us
  Pallas kernels  39.6 us (98%)
  between operations  0.66 us (2%)
    pallas_call x1, Pallas kernels, shards(): pl.pallas_call(functools.partial(kernel, n_gx, n_gy, cells), out_shape=pl...  38.9 us

profile of v4, /device:TPU:4, one launch (start us, length us, event | category | flops | bytes accessed | tf_op | source)
XLA Modules:
  0.0 40.2 jit_solution(4777245679196209752)
XLA Ops:
  0.7 38.9 %shard_map.46.tiles_ref = f32[256,128]{1,0:T(8,128)S(1)} custom-call(s32[1]{0:T(128)S(6)} %copy.5.shear_hbm, s32[4]{0:T(128)} %remap_hbm.1, s32[4]{0:T(128)} %frac_hbm.1, f32[8,2,4,508]{3,2,1,0:T(4,128)} %state_hbm.1), custom_call_target="tpu_custom_call" | custom-call | tf_op jit(solution)/shard_map/pallas_call | solution.py:768
  39.5 0.7 %shard_map.47 = f32[8,2,4,508]{3,2,1,0:T(4,128)} custom-call(f32[256,128]{1,0:T(8,128)S(1)} %shard_map.46.tiles_ref), custom_call_target="tpu_custom_call" | custom-call | tf_op jit(solution)/shard_map/pallas_call | solution.py:816

commit v5 on v4

--- a/solution.py
+++ b/solution.py
@@ -169,6 +169,8 @@
     framed_next,
     ghost_next,
     framed_face,
+    prior,
+    prior_face,
     fresh,
     fresh_edges,
     to_next,
@@ -350,11 +352,21 @@
 
         def whole(k, carry):
             t = lax.rem(k + (gy + half) * per, LINES)
-            send(held.at[t], line_place(line_own, t), 2, 2, middle, lax.div(t, per)).start()
+            owner = lax.div(t, per)
+            stays = lax.rem(t, ROWS) < 2
+
+            @pl.when(jnp.logical_not(stays & (owner == gy)))
+            def _():
+                send(held.at[t], line_place(line_own, t), 2, 2, jnp.where(stays, 0, middle), owner).start()
+
+            @pl.when(stays & (owner == gy))
+            def _():
+                pltpu.make_async_copy(held.at[t], line_place(line_own, t), recv_sems.at[2]).start()
+
             return carry
 
+        lax.fori_loop(0, STRIPS + 1, ghosts, 0)
         lax.fori_loop(0, LINES, whole, 0)
-        lax.fori_loop(0, STRIPS + 1, ghosts, 0)
         near_copy.wait_recv()
         send(near_face, line_place(line_face, 0), 13, 16 + 2 * per, middle, n_gy - 1).start()
 
@@ -401,13 +413,14 @@
         pages[page] = window(buffer, slot, n_gy, cells, amount, 3)
 
     def deliver(source, target, sem, arrived, x, y):
-        if x == "self":
-
-            @pl.when(y != gy)
+        if x == 0:
+            here = first_x & (y == gy)
+
+            @pl.when(jnp.logical_not(here))
             def _():
                 send(source, target, sem, arrived, 0, y).start()
 
-            @pl.when(y == gy)
+            @pl.when(here)
             def _():
                 pltpu.make_async_copy(source, target, recv_sems.at[arrived]).start()
 
@@ -416,6 +429,13 @@
 
     def hand(page, target, sem, arrived, x):
         everyone(lambda y: deliver(pages.at[page, y], target, sem, arrived, x, y))
+
+    def hand_prior(page, target, r):
+        for y in (0, half):
+            for plane in range(2):
+                part = pl.ds(4 * plane + 3, 1)
+                source = pages.at[page, (y - 1) % n_gy, part]
+                deliver(source, target.at[part], 9, 20 + 2 * per + r, 0, y)
 
     def hand_next(page, target, sem, arrived, x):
         def one(y):
@@ -448,12 +468,51 @@
         places.append((slot, lax.div(t, ROWS), lax.rem(t, ROWS)))
 
     def own_conditions(r, field, row):
-        inner = row < 3 + r
-        return inner, jnp.logical_and(inner, field == FACE_Y), (row == 3) & (field == FACE_X) & (r == 0)
+        inner = (row < 3 + r) & ((row < 2) == first_x)
+        edge = (row == 3) & (field == FACE_X) & (r == 0) & (gx == middle)
+        return inner, jnp.logical_and(inner, field == FACE_Y), edge
 
     def far_conditions(r, field, row):
         inner = row >= 2 + r
         return inner, jnp.logical_and(inner, field == FACE_Y)
+
+    def own_lines():
+        for slot, field, row in places:
+
+            @pl.when((row < 2) == first_x)
+            def _(slot=slot):
+                wait_bytes(line_own.at[slot, pl.ds(0, 8 * n_gy), :], recv_sems.at[2])
+
+        line_own[:, pl.ds(8 * n_gy, 8 * n_gy), :] = line_own[:, pl.ds(0, 8 * n_gy), :]
+        for slot, field, row in places:
+
+            def frame(r, carry, slot=slot, field=field, row=row):
+                inner, faces, edge = own_conditions(r, field, row)
+                amount = jnp.where(first_x, remap_own[r], remap_ref[r])
+                page = r * per + slot
+
+                @pl.when(jnp.logical_or(inner, edge))
+                def _():
+                    fill(page, line_own, slot, amount)
+
+                @pl.when(inner)
+                def _():
+                    hand(page, framed.at[r, field, row + 2 - r], 9, 11 + r, 0)
+                    hand_prior(page, prior.at[r, field, row + 2 - r], r)
+
+                @pl.when(edge)
+                def _():
+                    hand(page, framed_face.at[0], 9, 13, 0)
+                    hand_prior(page, prior_face.at[0], 0)
+
+                @pl.when(faces)
+                def _():
+                    start = 2 * (row + 2 - r)
+                    hand_next(page, lambda plane: framed_next.at[r, start + plane, pl.ds(0, 1)], 15, 18 + 2 * per + r, 0)
+
+                return carry
+
+            lax.fori_loop(0, 2, frame, 0)
 
     mine = jnp.where(lax.rem(gy, 2) == 0, lax.div(gy, 2), half + lax.div(gy, 2))
     ghost_places = []
@@ -536,6 +595,8 @@
             def _(slot=slot):
                 hand(4 * per + slot, last_face, 8, 5, last)
 
+        own_lines()
+
         for slot, field, row in places:
 
             @pl.when(row >= 2)
@@ -551,12 +612,13 @@
                     @pl.when(inner)
                     def _():
                         fill(page, line_far, slot, amount)
-                        hand(page, framed.at[r, field, row - 2 - r], 9, 11 + r, "self")
+                        hand(page, framed.at[r, field, row - 2 - r], 9, 11 + r, 0)
+                        hand_prior(page, prior.at[r, field, row - 2 - r], r)
 
                     @pl.when(faces)
                     def _():
                         start = 2 * (row - 2 - r)
-                        hand_next(page, lambda plane: framed_next.at[r, start + plane, pl.ds(0, 1)], 15, 18 + 2 * per + r, "self")
+                        hand_next(page, lambda plane: framed_next.at[r, start + plane, pl.ds(0, 1)], 15, 18 + 2 * per + r, 0)
 
                     return carry
 
@@ -567,34 +629,7 @@
 
     @pl.when(gx == middle)
     def _():
-        wait_bytes(line_own.at[:, pl.ds(0, 8 * n_gy), :], recv_sems.at[2])
-        line_own[:, pl.ds(8 * n_gy, 8 * n_gy), :] = line_own[:, pl.ds(0, 8 * n_gy), :]
-        for slot, field, row in places:
-
-            def frame(r, carry, slot=slot, field=field, row=row):
-                inner, faces, edge = own_conditions(r, field, row)
-                page = r * per + slot
-
-                @pl.when(jnp.logical_or(inner, edge))
-                def _():
-                    fill(page, line_own, slot, remap_ref[r])
-
-                @pl.when(inner)
-                def _():
-                    hand(page, framed.at[r, field, row + 2 - r], 9, 11 + r, 0)
-
-                @pl.when(edge)
-                def _():
-                    hand(page, framed_face.at[0], 9, 13, 0)
-
-                @pl.when(faces)
-                def _():
-                    start = 2 * (row + 2 - r)
-                    hand_next(page, lambda plane: framed_next.at[r, start + plane, pl.ds(0, 1)], 15, 18 + 2 * per + r, 0)
-
-                return carry
-
-            lax.fori_loop(0, 2, frame, 0)
+        own_lines()
 
         @pl.when(gy == spare)
         def _():
@@ -602,6 +637,7 @@
             line_face[0, pl.ds(8 * n_gy, 8 * n_gy), :] = line_face[0, pl.ds(0, 8 * n_gy), :]
             fill(5 * per, line_face, 0, remap_ref[1])
             hand(5 * per, framed_face.at[1], 9, 14, 0)
+            hand_prior(5 * per, prior_face.at[1], 1)
 
     expected = [jnp.logical_or(gx != middle, row >= 2) for _, _, row in places]
     for slot in range(per):
@@ -623,22 +659,50 @@
             everyone(lambda y: send(line_out.at[slot, y], target, 7, 7, partner, y).start())
 
     next_copy = send(to_next, from_previous, 12, 15, 0, right_y)
+    far_left = (gy == 0) | (gy == half)
+    sends_next = (gy != half - 1) & (gy != n_gy - 1)
+    prior_bytes = line_in.at[0, pl.ds(0, 82), :]
 
     @pl.when(first_x)
     def _():
+        def advance(fields, last, following):
+            fields = fields[:FACE_X] + [jnp.concatenate([fields[FACE_X], last[None]], axis=0)] + fields[FACE_Y:]
+            once = euler(fields, following)
+            twice = euler(once, ahead(once[FACE_Y], 1))
+            return [0.5 * (fields[field][2] + twice[field][0]) for field in range(8)]
+
         for r in range(2):
             wait_bytes(framed.at[r], recv_sems.at[11 + r])
             wait_bytes(framed_face.at[r], recv_sems.at[13 + r])
+            wait_bytes(framed_next.at[r, :, pl.ds(0, 1)], recv_sems.at[18 + 2 * per + r])
             fields = [framed[r, field] for field in range(8)]
-            fields[FACE_X] = jnp.concatenate([fields[FACE_X], framed_face[r][None]], axis=0)
-            wait_bytes(framed_next.at[r, :, pl.ds(0, 1)], recv_sems.at[18 + 2 * per + r])
-            once = euler(fields, next_faces(fields[FACE_Y], framed_next[r]))
-            twice = euler(once, ahead(once[FACE_Y], 1))
+            done = advance(fields, framed_face[r], next_faces(fields[FACE_Y], framed_next[r]))
             for field in range(8):
-                fresh[pl.ds(64 * r + 8 * field, 8), :] = 0.5 * (framed[r, field, 2] + twice[field][0])
-        to_next[...] = fresh[pl.ds(3, 32, stride=4), :]
-        next_copy.start()
-        next_copy.wait_recv()
+                fresh[pl.ds(64 * r + 8 * field, 8), :] = done[field]
+
+        @pl.when(sends_next)
+        def _():
+            to_next[...] = fresh[pl.ds(3, 32, stride=4), :]
+            next_copy.start()
+
+        @pl.when(far_left)
+        def _():
+            for r in range(2):
+                wait_bytes(prior_bytes, recv_sems.at[20 + 2 * per + r])
+                fields = [prior[r, field] for field in range(8)]
+                lanes = lax.broadcasted_iota(jnp.int32, fields[0].shape, 2)
+                chunks = lax.broadcasted_iota(jnp.int32, fields[0].shape, 1) % 4
+                follow = pltpu.roll(pltpu.roll(framed[r, FACE_Y], 123, 2), 3, 1)
+                following = jnp.where((chunks == 3) & (lanes == 127), follow, ahead(fields[FACE_Y], 1))
+                done = advance(fields, prior_face[r], following)
+                for field in range(8):
+                    fresh_edges[pl.ds(64 * r + 8 * field, 8), :] = done[field]
+            from_previous[...] = fresh_edges[pl.ds(3, 32, stride=4), :]
+
+        @pl.when(jnp.logical_not(far_left))
+        def _():
+            next_copy.wait_recv()
+
         reach = cells % 128 + 1
         fresh_edges[pl.ds(0, 32, stride=4), :] = pltpu.roll(from_previous[...], 129 - reach, 1)
 
@@ -687,6 +751,13 @@
         def _():
             wait_bytes(pages.at[page], send_sems.at[sem])
 
+    def left_prior(near):
+        for condition, rows in ((near, 2), (jnp.logical_not(near), 4)):
+
+            @pl.when(condition)
+            def _(rows=rows):
+                wait_bytes(line_in.at[0, pl.ds(0, rows), :], send_sems.at[9])
+
     def left_next(condition, one_less=0):
         @pl.when(condition)
         def _():
@@ -694,9 +765,19 @@
 
     @pl.when(first_x)
     def _():
-        wait_bytes(held, send_sems.at[2])
+        stayed = sum((row < 2).astype(jnp.int32) for _, _, row in places)
+        for count in range(per + 1):
+
+            @pl.when(stayed == count)
+            def _(count=count):
+                wait_bytes(held.at[pl.ds(0, LINES - count)], send_sems.at[2])
+
         wait_bytes(near_face, send_sems.at[13])
-        next_copy.wait_send()
+
+        @pl.when(sends_next)
+        def _():
+            next_copy.wait_send()
+
         count_own = sum((u <= STRIPS).astype(jnp.int32) for _, u, _ in ghost_places)
         for count in range(len(ghost_places) + 1):
 
@@ -716,6 +797,15 @@
                 @pl.when(inner)
                 def _(slot=slot, r=r):
                     wait_bytes(pages.at[(2 + r) * per + slot, pl.ds(0, n_gy - 1)], send_sems.at[9])
+                    left_prior(far_left)
+
+                inner, faces, _ = own_conditions(r, field, row)
+                left_next(faces, 1)
+
+                @pl.when(inner)
+                def _(slot=slot, r=r):
+                    wait_bytes(pages.at[r * per + slot, pl.ds(0, n_gy - 1)], send_sems.at[9])
+                    left_prior(far_left)
 
 
     @pl.when(gx == middle)
@@ -723,12 +813,18 @@
         @pl.when(gy == spare)
         def _():
             wait_bytes(pages.at[5 * per], send_sems.at[9])
+            left_prior(first_x)
 
         for slot, field, row in places:
             for r in range(2):
                 inner, faces, edge = own_conditions(r, field, row)
                 left(jnp.logical_or(inner, edge), r * per + slot, 9)
                 left_next(faces)
+
+                @pl.when(jnp.logical_or(inner, edge))
+                def _():
+                    left_prior(first_x)
+
 
     @pl.when(first_x)
     def _():
@@ -797,6 +893,8 @@
                 vmem(2, 10, 8, 128),
                 vmem(4, 8, 128),
                 vmem(2, 8, 128),
+                vmem(2, 8, 5, 8, 128),
+                vmem(2, 8, 128),
                 vmem(128, 128),
                 vmem(128, 128),
                 vmem(32, 128),
@@ -805,7 +903,7 @@
                 vmem(per, n_gy, 8, 128),
                 vmem(LINES, 8, 128),
                 pltpu.SemaphoreType.DMA((16,)),
-                pltpu.SemaphoreType.DMA((20 + 2 * per,)),
+                pltpu.SemaphoreType.DMA((22 + 2 * per,)),
                 pltpu.SemaphoreType.DMA((4,)),
                 pltpu.SemaphoreType.REGULAR((4,)),
             ],

time: 40.3 us -> 37.3 us (0.926)
  the two profiles are of different devices: /device:TPU:4 before, /device:TPU:1 now
where the time goes in v5:
time: 37.3 us; the launch traced here: 37 us
  Pallas kernels  36.3 us (97%)
  between operations  0.66 us (2%)
    pallas_call x1, Pallas kernels, shards(): pl.pallas_call(functools.partial(kernel, n_gx, n_gy, cells), out_shape=pl...  35.6 us

profile of v5, /device:TPU:1, one launch (start us, length us, event | category | flops | bytes accessed | tf_op | source)
XLA Modules:
  0.0 37.0 jit_solution(14512382218392363358)
XLA Ops:
  0.7 35.6 %shard_map.46.tiles_ref = f32[256,128]{1,0:T(8,128)S(1)} custom-call(s32[1]{0:T(128)S(6)} %copy.5.shear_hbm, s32[4]{0:T(128)} %remap_hbm.1, s32[4]{0:T(128)} %frac_hbm.1, f32[8,2,4,508]{3,2,1,0:T(4,128)} %state_hbm.1), custom_call_target="tpu_custom_call" | custom-call | tf_op jit(solution)/shard_map/pallas_call | solution.py:864
  36.3 0.7 %shard_map.47 = f32[8,2,4,508]{3,2,1,0:T(4,128)} custom-call(f32[256,128]{1,0:T(8,128)S(1)} %shard_map.46.tiles_ref), custom_call_target="tpu_custom_call" | custom-call | tf_op jit(solution)/shard_map/pallas_call | solution.py:914

commit v6 on v5

--- a/solution.py
+++ b/solution.py
@@ -476,7 +476,7 @@
         inner = row >= 2 + r
         return inner, jnp.logical_and(inner, field == FACE_Y)
 
-    def own_lines():
+    def own_lines(amounts_ref):
         for slot, field, row in places:
 
             @pl.when((row < 2) == first_x)
@@ -488,12 +488,11 @@
 
             def frame(r, carry, slot=slot, field=field, row=row):
                 inner, faces, edge = own_conditions(r, field, row)
-                amount = jnp.where(first_x, remap_own[r], remap_ref[r])
                 page = r * per + slot
 
                 @pl.when(jnp.logical_or(inner, edge))
                 def _():
-                    fill(page, line_own, slot, amount)
+                    fill(page, line_own, slot, amounts_ref[r])
 
                 @pl.when(inner)
                 def _():
@@ -595,7 +594,7 @@
             def _(slot=slot):
                 hand(4 * per + slot, last_face, 8, 5, last)
 
-        own_lines()
+        own_lines(remap_own)
 
         for slot, field, row in places:
 
@@ -629,7 +628,7 @@
 
     @pl.when(gx == middle)
     def _():
-        own_lines()
+        own_lines(remap_ref)
 
         @pl.when(gy == spare)
         def _():

time: 37.3 us -> 37.3 us (level)
  no operation moved by 1% of the time
where the time goes in v6:
time: 37.3 us; the launch traced here: 37 us
  Pallas kernels  36.3 us (97%)
  between operations  0.66 us (2%)
    pallas_call x1, Pallas kernels, shards(): pl.pallas_call(functools.partial(kernel, n_gx, n_gy, cells), out_shape=pl...  35.6 us

profile of v6, /device:TPU:1, one launch (start us, length us, event | category | flops | bytes accessed | tf_op | source)
XLA Modules:
  0.0 37.0 jit_solution(8725872135267934531)
XLA Ops:
  0.7 35.6 %shard_map.46.tiles_ref = f32[256,128]{1,0:T(8,128)S(1)} custom-call(s32[1]{0:T(128)S(6)} %copy.5.shear_hbm, s32[4]{0:T(128)} %remap_hbm.1, s32[4]{0:T(128)} %frac_hbm.1, f32[8,2,4,508]{3,2,1,0:T(4,128)} %state_hbm.1), custom_call_target="tpu_custom_call" | custom-call | tf_op jit(solution)/shard_map/pallas_call | solution.py:863
  36.3 0.7 %shard_map.47 = f32[8,2,4,508]{3,2,1,0:T(4,128)} custom-call(f32[256,128]{1,0:T(8,128)S(1)} %shard_map.46.tiles_ref), custom_call_target="tpu_custom_call" | custom-call | tf_op jit(solution)/shard_map/pallas_call | solution.py:913

commit v7 on v6

--- a/solution.py
+++ b/solution.py
@@ -594,7 +594,6 @@
             def _(slot=slot):
                 hand(4 * per + slot, last_face, 8, 5, last)
 
-        own_lines(remap_own)
 
         for slot, field, row in places:
 
@@ -622,6 +621,8 @@
                     return carry
 
                 lax.fori_loop(0, 2, frame, 0)
+
+        own_lines(remap_own)
 
     amounts.wait_recv()
     levels.wait_recv()

time: 37.3 us -> 37.3 us (level)
  no operation moved by 1% of the time
where the time goes in v7:
time: 37.3 us; the launch traced here: 37 us
  Pallas kernels  36.3 us (97%)
  between operations  0.66 us (2%)
    pallas_call x1, Pallas kernels, shards(): pl.pallas_call(functools.partial(kernel, n_gx, n_gy, cells), out_shape=pl...  35.6 us

profile of v7, /device:TPU:1, one launch (start us, length us, event | category | flops | bytes accessed | tf_op | source)
XLA Modules:
  0.0 37.0 jit_solution(9976377235008354871)
XLA Ops:
  0.7 35.6 %shard_map.46.tiles_ref = f32[256,128]{1,0:T(8,128)S(1)} custom-call(s32[1]{0:T(128)S(6)} %copy.5.shear_hbm, s32[4]{0:T(128)} %remap_hbm.1, s32[4]{0:T(128)} %frac_hbm.1, f32[8,2,4,508]{3,2,1,0:T(4,128)} %state_hbm.1), custom_call_target="tpu_custom_call" | custom-call | tf_op jit(solution)/shard_map/pallas_call | solution.py:864
  36.3 0.7 %shard_map.47 = f32[8,2,4,508]{3,2,1,0:T(4,128)} custom-call(f32[256,128]{1,0:T(8,128)S(1)} %shard_map.46.tiles_ref), custom_call_target="tpu_custom_call" | custom-call | tf_op jit(solution)/shard_map/pallas_call | solution.py:914
